TPU v7x, 256 devices: a whole 4x4x8 slice. The times are simulated.
256 devices in a mesh: grp: 32 (over x, y, core), tp: 8 (over z).
Axes of the slice: x: 4, y: 4, z: 8, core: 2. Of those that a mesh axis runs over, the one named last changes fastest.
Arguments:
- hidden_in: bfloat16 [512, 2048], P('grp'), may hold values from -6 to 6
- norm_gain: bfloat16 [2048], replicated, may hold values from 0.099609375 to 1.8984375
- w_query: bfloat16 [2048, 2048], P(None, 'tp'), may hold values from -0.125 to 0.125
- w_keyval: bfloat16 [2048, 512], P(None, 'tp'), may hold values from -0.125 to 0.125
- w_output: bfloat16 [2048, 2048], P('tp'), may hold values from -0.125 to 0.125
- prefix_cache: bfloat16 [64, 512, 512], P('grp', 'tp'), may hold values from -130 to 130
- private_cache: bfloat16 [512, 512, 512], P('grp', 'tp'), may hold values from -130 to 130
- node_parent: int32 [64], replicated, may hold values from 0 to 3, as said below
- node_length: int32 [64], replicated, may hold values from 1 to 512, as said below
- request_node: int32 [512], replicated, may hold values from 4 to 63, as said below
- private_length: int32 [512], P('grp'), may hold values from 0 to 512, as said below
Outputs:
- hidden_out: bfloat16 [512, 2048], P('grp', 'tp')
- new_keyval: bfloat16 [512, 512], P('grp', 'tp')
Inputs may be any that keep to these rules, and one draw needn't show every extreme that they name: `node_parent`: nodes 0 to 3 are the tenants' roots and are their own parents; every other node's parent is a root, and every root has a child. `request_node`: request r belongs to tenant r // 128; its node is a non-root node whose parent is that tenant's root. `node_length`: the longest node has exactly 512 used slots. `private_length`: some request has exactly 512 used slots.
All inputs are finite; a program needn't handle non-finite values.
Results may differ from a plain program's by a relative error of at most 0.023.
Values may be sent and summed in bfloat16 or wider, within the bound.
A program may use at most 128 MiB of HBM per device.

v0:
```python
import math

import jax
import jax.numpy as jnp
from jax import lax
from jax.sharding import PartitionSpec as P

HEADS = 32
KV_HEADS = 4
HEAD_DIM = 64
TENANTS = 4


def combined_all(x, axis, combine):
    everything = jax.tree.map(
        lambda part, kind: lax.all_gather(part.astype(kind), axis),
        x,
        (jnp.bfloat16, jnp.bfloat16, jnp.bfloat16),
    )

    def take(k):
        return jax.tree.map(lambda part, own: part[k].astype(own.dtype), everything, x)

    return lax.fori_loop(
        1, lax.axis_size(axis), lambda k, so_far: combine(so_far, take(k)), take(0)
    )


def rms_norm(values, scale_gain):
    floats = values.astype(jnp.float32)
    spread = jnp.mean(floats * floats, axis=-1, keepdims=True)
    return (floats * lax.rsqrt(spread + 1e-05) * scale_gain.astype(jnp.float32)).astype(
        jnp.bfloat16
    )


def rotate(head_rows, position):
    half_dim = head_rows.shape[-1] // 2
    freq_index = jnp.arange(half_dim, dtype=jnp.float32)
    frequency = jnp.exp(freq_index * (-2.0 * math.log(10000.0) / head_rows.shape[-1]))
    angles = position[:, None, None] * frequency[None, None, :]
    cosine = jnp.cos(angles)
    sine_part = jnp.sin(angles)
    front_half = head_rows[..., :half_dim]
    back_half = head_rows[..., half_dim:]
    return jnp.concatenate(
        [front_half * cosine - back_half * sine_part, back_half * cosine + front_half * sine_part],
        axis=-1,
    )


def softmax_part(queries, key_rows, value_rows, valid, shared):
    row_count = queries.shape[0]
    grouped = queries.reshape(row_count, KV_HEADS, HEADS // KV_HEADS, HEAD_DIM)
    if shared:
        scores = jnp.einsum("nkgd,lkd->nkgl", grouped, key_rows, preferred_element_type=jnp.float32)
    else:
        scores = jnp.einsum(
            "nkgd,nlkd->nkgl", grouped, key_rows, preferred_element_type=jnp.float32
        )
    scores = scores * HEAD_DIM ** (-0.5)
    usable = valid[:, None, None, :]
    scores = jnp.where(usable, scores, -jnp.inf)
    maxima = jnp.maximum(jnp.max(scores, axis=-1), -1e30)
    weights = jnp.where(usable, jnp.exp(scores - maxima[..., None]), 0.0)
    totals = jnp.sum(weights, axis=-1)
    rounded = weights.astype(jnp.bfloat16)
    if shared:
        weighted = jnp.einsum(
            "nkgl,lkd->nkgd", rounded, value_rows, preferred_element_type=jnp.float32
        )
    else:
        weighted = jnp.einsum(
            "nkgl,nlkd->nkgd", rounded, value_rows, preferred_element_type=jnp.float32
        )
    return (weighted, maxima, totals)


def merge_pair(left_part, right_part):
    left_sum, left_max, left_total = left_part
    right_sum, right_max, right_total = right_part
    upper = jnp.maximum(left_max, right_max)
    left_factor = jnp.exp(left_max - upper)
    right_factor = jnp.exp(right_max - upper)
    merged_sum = left_sum * left_factor[..., None] + right_sum * right_factor[..., None]
    return (merged_sum, upper, left_total * left_factor + right_total * right_factor)


def add_token(weighted, maxima, totals, token_score, token_value, form):
    upper = jnp.maximum(maxima, token_score)
    former = jnp.exp(maxima - upper)
    fresh = jnp.exp(token_score - upper)
    summed = weighted * former[..., None] + jnp.einsum(
        form, fresh.astype(jnp.bfloat16), token_value, preferred_element_type=jnp.float32
    )
    return summed / (totals * former + fresh)[..., None]


def on_device(
    hidden_in,
    norm_gain,
    w_query,
    w_keyval,
    w_output,
    prefix_cache,
    private_cache,
    node_parent,
    node_length,
    request_node,
    private_length,
):
    grp_index = lax.axis_index("grp")
    tp_index = lax.axis_index("tp")
    req_dev = hidden_in.shape[0]
    total_req = request_node.shape[0]
    per_tenant = total_req // TENANTS
    share_count = HEADS // KV_HEADS
    key_width = KV_HEADS * HEAD_DIM
    local_heads = w_query.shape[1] // HEAD_DIM
    local_kv = w_keyval.shape[1] // HEAD_DIM
    slice_width = local_heads * HEAD_DIM
    node_dev = prefix_cache.shape[0]
    local_len = prefix_cache.shape[1]
    priv_len = private_cache.shape[1]
    scale_factor = HEAD_DIM ** (-0.5)
    normed = rms_norm(hidden_in, norm_gain)
    query = jnp.dot(normed, w_query, preferred_element_type=jnp.float32)
    keyval = jnp.dot(normed, w_keyval, preferred_element_type=jnp.float32)
    own_mid = lax.dynamic_slice_in_dim(request_node, grp_index * req_dev, req_dev)
    own_root = node_parent[own_mid]
    position = (node_length[own_root] + node_length[own_mid] + private_length).astype(jnp.float32)
    query_rot = (
        rotate(query.reshape(req_dev, local_heads, HEAD_DIM), position)
        .reshape(req_dev, slice_width)
        .astype(jnp.bfloat16)
    )
    kv_rows = keyval.reshape(req_dev, local_kv, HEAD_DIM)
    is_key = tp_index * local_kv + jnp.arange(local_kv) < KV_HEADS
    new_keyval = (
        jnp.where(is_key[None, :, None], rotate(kv_rows, position), kv_rows)
        .reshape(req_dev, local_kv * HEAD_DIM)
        .astype(jnp.bfloat16)
    )
    query_all, keyval_all = (
        lax.all_gather(query_rot, "tp", axis=1, tiled=True),
        lax.all_gather(new_keyval, "tp", axis=1, tiled=True),
    )
    everyone = lax.all_gather(query_all, "grp", axis=0, tiled=True)
    private_valid = (tp_index * priv_len + jnp.arange(priv_len))[None, :] < private_length[:, None]
    private_keys = private_cache[:, :, :key_width].reshape(req_dev, priv_len, KV_HEADS, HEAD_DIM)
    private_values = private_cache[:, :, key_width:].reshape(req_dev, priv_len, KV_HEADS, HEAD_DIM)
    private_part = softmax_part(query_all, private_keys, private_values, private_valid, False)
    slot_positions = tp_index * local_len + jnp.arange(local_len)
    node_parts = []
    for node_slot in range(node_dev):
        node_id = grp_index * node_dev + node_slot
        is_root = node_id < TENANTS
        member = jnp.where(is_root, node_parent[request_node] == node_id, request_node == node_id)
        order_key = jnp.where(member, 0, total_req) + jnp.arange(total_req)
        picked = lax.top_k(-order_key, per_tenant)[1]
        filled = jnp.arange(per_tenant) < jnp.sum(member.astype(jnp.int32))
        chosen = jnp.take(everyone, picked, axis=0)
        node_rows = prefix_cache[node_slot]
        node_keys = node_rows[:, :key_width].reshape(local_len, KV_HEADS, HEAD_DIM)
        node_values = node_rows[:, key_width:].reshape(local_len, KV_HEADS, HEAD_DIM)
        node_valid = (slot_positions < node_length[node_id])[None, :]
        weighted, maxima, totals = softmax_part(chosen, node_keys, node_values, node_valid, True)
        level_slot = jnp.where(is_root, 0, 1)
        node_parts.append((picked, filled, level_slot, weighted, maxima, totals))
    sum_rows = jnp.zeros((total_req, 2, HEADS * HEAD_DIM), jnp.float32)
    max_rows = jnp.zeros((total_req, 2, HEADS), jnp.float32)
    total_rows = jnp.zeros((total_req, 2, HEADS), jnp.float32)
    for entry in node_parts:
        picked, filled, level_slot, weighted, maxima, totals = entry
        keep = filled[:, None]
        sum_rows = sum_rows.at[picked, level_slot].add(
            jnp.where(keep, weighted.reshape(per_tenant, HEADS * HEAD_DIM), 0.0)
        )
        max_rows = max_rows.at[picked, level_slot].add(
            jnp.where(keep, maxima.reshape(per_tenant, HEADS), 0.0)
        )
        total_rows = total_rows.at[picked, level_slot].add(
            jnp.where(keep, totals.reshape(per_tenant, HEADS), 0.0)
        )
    back_sum, back_max, back_total = (
        lax.psum_scatter(sum_rows, "grp", scatter_dimension=0, tiled=True),
        lax.psum_scatter(max_rows, "grp", scatter_dimension=0, tiled=True),
        lax.psum_scatter(total_rows, "grp", scatter_dimension=0, tiled=True),
    )
    stat_shape = (req_dev, 2, KV_HEADS, share_count)
    back_sum = back_sum.reshape(req_dev, 2, KV_HEADS, share_count, HEAD_DIM)
    back_max = back_max.reshape(stat_shape)
    back_total = back_total.reshape(stat_shape)
    root_part = (back_sum[:, 0], back_max[:, 0], back_total[:, 0])
    mid_part = (back_sum[:, 1], back_max[:, 1], back_total[:, 1])
    local_sum, local_max, local_total = merge_pair(merge_pair(root_part, mid_part), private_part)
    full_sum, full_max, full_total = combined_all(
        (local_sum, local_max, local_total), "tp", merge_pair
    )
    grouped = query_all.reshape(req_dev, KV_HEADS, share_count, HEAD_DIM)
    token_keys = keyval_all[:, :key_width].reshape(req_dev, KV_HEADS, HEAD_DIM)
    token_values = keyval_all[:, key_width:].reshape(req_dev, KV_HEADS, HEAD_DIM)
    token_score = (
        jnp.einsum("nkgd,nkd->nkg", grouped, token_keys, preferred_element_type=jnp.float32)
        * scale_factor
    )
    attention_all = (
        add_token(full_sum, full_max, full_total, token_score, token_values, "nkg,nkd->nkgd")
        .reshape(req_dev, HEADS * HEAD_DIM)
        .astype(jnp.bfloat16)
    )
    attention = lax.dynamic_slice_in_dim(attention_all, tp_index * slice_width, slice_width, 1)
    projected = jnp.dot(attention, w_output, preferred_element_type=jnp.float32)
    summed = lax.psum_scatter(
        projected.astype(jnp.bfloat16), "tp", scatter_dimension=1, tiled=True
    ).astype(jnp.float32)
    out_width = summed.shape[1]
    residual = lax.dynamic_slice_in_dim(hidden_in, tp_index * out_width, out_width, 1).astype(
        jnp.float32
    )
    hidden_out = (summed + residual).astype(jnp.bfloat16)
    return (hidden_out, new_keyval)


def solution(mesh):
    placed = (
        P("grp", None),
        P(),
        P(None, "tp"),
        P(None, "tp"),
        P("tp", None),
        P("grp", "tp", None),
        P("grp", "tp", None),
        P(),
        P(),
        P(),
        P("grp"),
    )
    return jax.shard_map(
        on_device,
        mesh=mesh,
        in_specs=placed,
        out_specs=(P("grp", "tp"), P("grp", "tp")),
        check_vma=False,
    )
```

profile of v0, /device:TPU:1, one launch (start us, length us, event | category | flops | bytes accessed | tf_op | source)
XLA Modules:
  0.0 471.5 jit_solution(16032584762213668495)
XLA Ops:
  7.3 0.8 compare_select_fusion.3
  8.1 1.3 gather_fusion
  9.4 1.3 gather_fusion.2
  10.7 1.3 gather_fusion.1
  12.1 0.7 convert_element_type.137
  12.8 1.0 fusion.32
  13.8 1.6 fusion.59
  15.4 0.7 add_convert_fusion.2
  16.5 24.9 %all_gather.23 = bf16[16,2048]{1,0:T(8,128)(2,1)} all-gather(bf16[16,256]{1,0:T(8,128)(2,1)S(1)} %convert_element_type.140), channel_id=1, replica_groups=mesh['grp'=32,'tp'=8] {'tp'}, dimensions={1}, use_global_device_ids=true | all-gather | bytes 73728 | tf_op jit(solution)/shard_map/all_gather | solution.py:145
  41.5 0.9 slice_bitcast_fusion.2
  42.8 1.6 fusion.90
  44.4 2.1 fusion.87
  46.5 2.1 fusion.88
  48.6 2.1 fusion.89
  50.7 41.3 %convert_reduce_fusion = (s32[]{:T(128)}, pred[512]{0:T(512)(128)(4,1)S(1)}, s32[512]{0:T(512)S(1)}) fusion(s32[512]{0:T(512)} %param.24, s32[]{:T(128)S(6)} %add.231, pred[]{:T(512)S(6)} %lt.150, s32[]{:T(128)} %bitcast.67, s32[]{:T(128)} %bitcast.66, s32[]{:T(128)} %bitcast.65, s32[]{:T(128)} %bitcast.64, s32[]{:T(128)} %bitcast.63, s32[]{:T(128)} %bitcast.62, ...), kind=kLoop, calls=%fused_computation.153 | loop fusion | flops 68607 | bytes 4873 | tf_op jit(solution)/shard_map/reduce_sum | solution.py:161
  92.0 1.3 convert_reduce_fusion.1
  93.3 3.8 top_k.17
  97.1 3.8 top_k.24
  100.9 1.3 fusion.86
  102.2 0.6 iota_compare_fusion.1
  102.9 0.6 iota_compare_fusion
  103.5 1.3 broadcast_compare_fusion.1
  104.9 4.3 gather_fusion.3
  109.2 2.0 broadcast_select_fusion.3
  111.2 2.0 copy.74
  113.2 1.3 fusion.91
  114.6 0.9 copy-done.2
  115.9 1.7 gather_fusion.4
  117.6 1.2 broadcast_select_fusion.2
  119.1 0.3 fusion.92
  119.7 0.3 copy-done.9
  120.3 1.6 fusion.18
  121.9 1.3 copy.77
  123.3 1.4 broadcast_select_fusion.1
  124.6 2.1 fusion.16
  126.7 1.6 copy.81
  128.3 1.1 broadcast_select_fusion
  129.5 6.8 %scatter_fusion.4 = f32[512,2,32]{2,1,0:T(2,128)S(1)} fusion(f32[512,2,32]{2,1,0:T(2,128)S(1)} %broadcast.255.clone.1, s32[128]{0:T(128)S(1)} %fusion.77, f32[128,32]{1,0:T(8,128)S(1)} %copy.94), kind=kCustom, calls=%fused_computation.9 | custom fusion | flops 4096 | bytes 50176 | tf_op jit(solution)/shard_map/scatter-add | solution.py:182
  136.5 6.6 %scatter_fusion.2 = f32[512,2,32]{2,1,0:T(2,128)S(1)} fusion(f32[512,2,32]{2,1,0:T(2,128)S(1)} %broadcast.255.clone, s32[128]{0:T(128)S(1)} %fusion.77, f32[128,32]{1,0:T(8,128)S(1)} %copy.83), kind=kCustom, calls=%fused_computation.7 | custom fusion | flops 4096 | bytes 50176 | tf_op jit(solution)/shard_map/scatter-add | solution.py:179
  143.1 6.6 %scatter_fusion.5 = f32[512,2,32]{2,1,0:T(2,128)S(1)} fusion(f32[512,2,32]{2,1,0:T(2,128)S(1)} %scatter_fusion.4, s32[128]{0:T(128)S(1)} %fusion.78, f32[128,32]{1,0:T(8,128)S(1)} %copy.95), kind=kCustom, calls=%fused_computation.10 | custom fusion | flops 4096 | bytes 50176 | tf_op jit(solution)/shard_map/scatter-add | solution.py:182
  149.7 6.6 %scatter_fusion.3 = f32[512,2,32]{2,1,0:T(2,128)S(1)} fusion(f32[512,2,32]{2,1,0:T(2,128)S(1)} %scatter_fusion.2, s32[128]{0:T(128)S(1)} %fusion.78, f32[128,32]{1,0:T(8,128)S(1)} %copy.84), kind=kCustom, calls=%fused_computation.8 | custom fusion | flops 4096 | bytes 50176 | tf_op jit(solution)/shard_map/scatter-add | solution.py:179
  156.3 7.5 %broadcast_in_dim.180 = f32[512,2,2048]{2,1,0:T(2,128)} broadcast(f32[]{:T(128)} %constant.85.clone.1), dimensions={} | broadcast | bytes 8388612 | tf_op jit(solution)/shard_map/broadcast_in_dim | solution.py:170
  163.8 21.2 %scatter_fusion = f32[512,2,2048]{2,1,0:T(2,128)} fusion(f32[512,2,2048]{2,1,0:T(2,128)} %broadcast_in_dim.180, s32[128]{0:T(128)S(1)} %fusion.77, f32[128,2048]{1,0:T(8,128)S(1)} %broadcast_select_fusion.1), kind=kCustom, calls=%fused_computation.5 | custom fusion | flops 262144 | bytes 3146752 | tf_op jit(solution)/shard_map/scatter-add | solution.py:176
  185.0 22.7 %scatter_fusion.1 = f32[512,2,2048]{2,1,0:T(2,128)} fusion(f32[512,2,2048]{2,1,0:T(2,128)} %scatter_fusion, s32[128]{0:T(128)S(1)} %fusion.78, f32[128,2048]{1,0:T(8,128)} %broadcast_select_fusion), kind=kCustom, calls=%fused_computation.6 | custom fusion | flops 262144 | bytes 3146752 | tf_op jit(solution)/shard_map/scatter-add | solution.py:176
  207.9 0.7 copy-done.6
  209.1 0.4 reshape.467
  209.7 0.7 fusion.93
  210.5 1.4 reshape.468
  211.9 1.2 fusion.57
  213.3 18.9 %all-gather.1 = bf16[8,64,16]{1,2,0:T(8,128)(2,1)S(1)} all-gather(bf16[1,64,16]{1,2,0:T(8,128)(2,1)S(1)} %bitcast.283), channel_id=1, replica_groups=mesh['grp'=32,'tp'=8] {'tp'}, dimensions={0}, use_global_device_ids=true | all-gather | bytes 18432 | tf_op jit(solution)/shard_map/all_gather | solution.py:146
  232.5 0.6 dynamic-slice
  233.9 113.0 %all-reduce.8.cloned.1.call-done = (f32[512,2,2048]{2,1,0:T(2,128)}, f32[512,2,32]{2,1,0:T(2,128)}, f32[512,2,32]{2,1,0:T(2,128)}) async-done(((f32[512,2,2048]{2,1,0:T(2,128)}, f32[512,2,32]{2,1,0:T(2,128)}, f32[512,2,32]{2,1,0:T(2,128)}), (f32[512,2,2048]{2,1,0:T(2,128)}, f32[512,2,32]{2,1,0:T(2,128)}, f32[512,2,32]{2,1,0:T(2,128)})) %all-reduce.8.cloned.1.call-update) | async-done | bytes 8650768
  347.0 0.7 constant_dynamic-slice_fusion.3
  347.9 0.3 fusion.30
  348.3 0.7 constant_dynamic-slice_fusion.2
  349.1 19.8 %all_gather.28 = bf16[8,16,4,8]{1,3,2,0:T(8,128)(2,1)S(1)} all-gather(bf16[1,16,4,8]{1,3,2,0:T(8,128)(2,1)S(1)} %fusion.49), channel_id=1, replica_groups=mesh['grp'=32,'tp'=8] {'tp'}, dimensions={0}, use_global_device_ids=true | all-gather | bytes 9216 | tf_op jit(solution)/shard_map/all_gather | solution.py:16
  369.2 1.0 constant_dynamic-slice_fusion.4
  370.7 1.7 fusion.9
  372.4 21.4 %all-gather = bf16[128,4,8,64]{3,2,1,0:T(8,128)(2,1)S(1)} all-gather(bf16[16,4,8,64]{3,2,1,0:T(8,128)(2,1)S(1)} %fusion.9), channel_id=2, replica_groups=mesh['grp'=32,'tp'=8] {'tp'}, dimensions={0}, use_global_device_ids=true | all-gather | bytes 589824 | tf_op jit(solution)/shard_map/all_gather | solution.py:16
  393.8 18.9 %all_gather.27 = bf16[8,16,4,8]{1,3,2,0:T(8,128)(2,1)S(1)} all-gather(bf16[1,16,4,8]{1,3,2,0:T(8,128)(2,1)S(1)} %fusion.56), channel_id=1, replica_groups=mesh['grp'=32,'tp'=8] {'tp'}, dimensions={0}, use_global_device_ids=true | all-gather | bytes 9216 | tf_op jit(solution)/shard_map/all_gather | solution.py:16
  412.7 3.9 while.19
  417.2 0.9 convolution_convert_fusion
  418.1 45.6 %reduce-scatter.2.cloned.1.call-done = bf16[16,256]{1,0:T(8,128)(2,1)} async-done(((bf16[16,2048]{1,0:T(8,128)(2,1)}), bf16[16,256]{1,0:T(8,128)(2,1)}) %reduce-scatter.2.cloned.1.call-update) | async-done | bytes 8208 | tf_op jit(solution)/shard_map/reduce_scatter | solution.py:214
  463.7 1.3 add_convert_fusion.1
  (159 shorter events, 9.6 us)
Async XLA Ops:
  7.2 410.0 %copy-start = (bf16[256,2048]{1,0:T(8,128)(2,1)S(1)}, bf16[256,2048]{1,0:T(8,128)(2,1)}, u32[]{:S(2)}) copy-start(bf16[256,2048]{1,0:T(8,128)(2,1)} %param.19) | copy-start | bytes 3145732
  7.2 97.7 %all-gather.4.cloned.1.call-start = ((), (), s32[]{:S(2)}) async-start(), calls=%async_computation.1 | async-start | bytes 2162688 | tf_op jit(solution)/shard_map/all_gather | solution.py:148
  7.2 97.6 %copy-start.18 = (f32[32]{0:T(128)}, f32[32]{0:T(128)S(1)}, u32[]{:S(2)}) copy-start(f32[32]{0:T(128)S(1)} %multiply_exponential_fusion) | copy-start | bytes 388
  13.7 1.6 copy-start.21
  16.1 88.8 %copy-start.13 = (f32[16]{0:T(128)}, f32[16]{0:T(128)S(1)}, u32[]{:S(2)}) copy-start(f32[16]{0:T(128)S(1)} %add_convert_fusion.2) | copy-start | bytes 196
  41.4 305.6 %all-reduce.8.cloned.1.call-start = ((), (), s32[]{:S(2)}) async-start(), calls=%async_computation.3 | async-start | bytes 18874368
  102.9 16.5 %copy-start.17 = (pred[128]{0:T(512)(128)(4,1)}, pred[128]{0:T(512)(128)(4,1)S(1)}, u32[]{:S(2)}) copy-start(pred[128]{0:T(512)(128)(4,1)S(1)} %iota_compare_fusion.1) | copy-start | bytes 388
  103.5 16.2 %copy-start.15 = (pred[128]{0:T(512)(128)(4,1)}, pred[128]{0:T(512)(128)(4,1)S(1)}, u32[]{:S(2)}) copy-start(pred[128]{0:T(512)(128)(4,1)S(1)} %iota_compare_fusion) | copy-start | bytes 388
  104.8 9.8 %copy-start.12 = (pred[64]{0:T(512)(128)(4,1)}, pred[64]{0:T(512)(128)(4,1)S(1)}, u32[]{:S(2)}) copy-start(pred[64]{0:T(512)(128)(4,1)S(1)} %get-tuple-element.351) | copy-start | bytes 196
  104.8 14.6 %copy-start.11 = (pred[64]{0:T(512)(128)(4,1)}, pred[64]{0:T(512)(128)(4,1)S(1)}, u32[]{:S(2)}) copy-start(pred[64]{0:T(512)(128)(4,1)S(1)} %get-tuple-element.350) | copy-start | bytes 196
  104.9 11.0 %copy-start.1 = (bf16[512,2048]{1,0:T(8,128)(2,1)S(1)}, bf16[512,2048]{1,0:T(8,128)(2,1)}, u32[]{:S(2)}) copy-start(bf16[512,2048]{1,0:T(8,128)(2,1)} %all-gather.4.cloned.1.call-done) | copy-start | bytes 6291460
  114.6 1.0 copy-start.2
  114.6 1.2 copy-start.8
  119.4 0.6 copy-start.9
  121.9 6.3 %copy-start.16 = (pred[128]{0:T(512)(128)(4,1)S(1)}, pred[128]{0:T(512)(128)(4,1)}, u32[]{:S(2)}) copy-start(pred[128]{0:T(512)(128)(4,1)} %copy-done.15) | copy-start | bytes 388
  149.7 35.4 %copy-start.3 = (f32[512,2,32]{2,1,0:T(2,128)}, f32[512,2,32]{2,1,0:T(2,128)S(1)}, u32[]{:S(2)}) copy-start(f32[512,2,32]{2,1,0:T(2,128)S(1)} %scatter_fusion.5) | copy-start | bytes 393220
  156.3 28.8 %copy-start.4 = (f32[512,2,32]{2,1,0:T(2,128)}, f32[512,2,32]{2,1,0:T(2,128)S(1)}, u32[]{:S(2)}) copy-start(f32[512,2,32]{2,1,0:T(2,128)S(1)} %scatter_fusion.3) | copy-start | bytes 393220
  207.8 0.8 copy-start.6
  207.8 1.3 copy-start.5
  207.8 1.8 copy-start.20
  207.8 4.2 copy-start.7
  207.8 4.2 copy-start.22
  207.8 5.3 %copy-start.14 = (f32[16]{0:T(128)S(1)}, f32[16]{0:T(128)}, u32[]{:S(2)}) copy-start(f32[16]{0:T(128)} %copy-done.13) | copy-start | bytes 196
  207.8 5.3 %copy-start.19 = (f32[32]{0:T(128)S(1)}, f32[32]{0:T(128)}, u32[]{:S(2)}) copy-start(f32[32]{0:T(128)} %copy-done.18) | copy-start | bytes 388
  207.8 24.7 %copy-start.23 = (u32[256]{0:T(256)S(1)}, u32[256]{0:T(256)}, u32[]{:S(2)}) copy-start(u32[256]{0:T(256)} %constant.274) | copy-start | bytes 3076
  207.8 255.8 %reduce-scatter.2.cloned.1.call-start = ((), (), s32[]{:S(2)}) async-start(), calls=%async_computation.2 | async-start | bytes 73728 | tf_op jit(solution)/shard_map/reduce_scatter | solution.py:214
  213.3 204.7 %copy-start.10 = (bf16[16,64]{1,0:T(8,128)(2,1)}, bf16[16,64]{1,0:T(8,128)(2,1)S(1)}, u32[]{:S(2)}) copy-start(bf16[16,64]{1,0:T(8,128)(2,1)S(1)} %fusion.71) | copy-start | bytes 6148
Sparse Core Ops, SparseCore 0:
  41.5 55.1 all-gather.3
  208.0 138.9 all-reduce.7
  418.2 45.4 reduce-scatter.1
where the time goes:
time: 478 us; the launch traced here: 471 us
  waiting for transfers between devices  159 us (33%)
  other arithmetic  137 us (29%)
  blocking collectives  104 us (22%)
  local copies, waits for them, and re-layouts  44.5 us (9%)
  between operations  15.1 us (3%)
  matrix products  11.6 us (2%)
    unnamed x4, waiting for transfers between devices  113 us
    all_gather x3, blocking collectives, combined_all(): lax.all_gather(part.astype(kind), axis)  60 us
    reduce_scatter x1, waiting for transfers between devices, on_device(): lax.psum_scatter(projected.astype(jnp.bfloat16), 'tp', scatter_dimension=...  45.6 us
    scatter-add x2, other arithmetic, on_device(): sum_rows.at[picked, level_slot]  44 us
    reduce_sum x2, other arithmetic, on_device(): filled = jnp.arange(per_tenant) < jnp.sum(member.astype(jnp.int32))  42.6 us
    all_gather x1, blocking collectives, on_device(): lax.all_gather(query_rot, 'tp', axis=1, tiled=True)  24.9 us
    all_gather x1, blocking collectives, on_device(): lax.all_gather(new_keyval, 'tp', axis=1, tiled=True)  18.9 us
    scatter-add x2, other arithmetic, on_device(): total_rows.at[picked, level_slot]  13.4 us
  transfers between devices with their start and end apart: 3, of which 2 were waited for; matrix products, arithmetic and copies ran while one was open for 15% of the time, Pallas kernels for 0%

commit v1 on v0

v1 whole, which is shorter than its diff:
```python
import math

import jax
import jax.numpy as jnp
from jax import lax
from jax.experimental import pallas as pl
from jax.experimental.pallas import tpu as pltpu
from jax.sharding import PartitionSpec as P

MESH = pl.DeviceIdType.MESH
F32 = jnp.float32
BF16 = jnp.bfloat16
HEADS = 32
KV_HEADS = 4
HEAD_DIM = 64
REQ = 16
SLOTS = 64
ROWS = HEADS * REQ
KW = KV_HEADS * HEAD_DIM
LOW = -1e30


def dot(a, b):
    return jnp.dot(a, b, preferred_element_type=F32)


def dot_t(a, b):
    return lax.dot_general(a, b, (((1,), (1,)), ((), ())), preferred_element_type=F32)


def three_parts(value):
    first = value.astype(BF16).astype(F32)
    rest = value - first
    second = rest.astype(BF16).astype(F32)
    third = (rest - second).astype(BF16).astype(F32)
    return first, second, third


def rope_tables(position):
    lane = lax.broadcasted_iota(jnp.int32, (REQ, 128), 1)
    index = (lane % (HEAD_DIM // 2)).astype(F32)
    frequency = jnp.exp(index * (-2.0 * math.log(10000.0) / HEAD_DIM))
    angle = position * frequency
    front = lane % HEAD_DIM < HEAD_DIM // 2
    sine = jnp.sin(angle)
    return jnp.cos(angle), jnp.where(front, -sine, sine), front


def rope(block, tables):
    cosine, sine, front = tables
    half = HEAD_DIM // 2
    swapped = jnp.where(front, pltpu.roll(block, 128 - half, 1), pltpu.roll(block, half, 1))
    return block * cosine + swapped * sine


def kernel(
    hid, gain, wq, wkv, wo, prefix, private, parent, nlen, reqnode, plen,
    out_h, out_kv,
    v_hid, v_gain, v_wq, v_wkv, v_wo, v_priv, nodes,
    q_all, kv_send, kv_recv, part_send, part_recv, rs_send, rs_recv,
    l_sem, a_send, a_recv, d_send, d_recv, s_send, s_recv, z_send, z_recv, kv_ss, kv_rs,
):
    g = lax.axis_index("grp")
    t = lax.axis_index("tp")
    x, y, c = g // 8, (g // 2) % 4, g % 2

    def group(xx, yy, cc):
        return (xx * 4 + yy) * 2 + cc

    def chunk(xx, yy, cc):
        return nodes.at[pl.ds(group(xx, yy, cc) * 2, 2)]

    def half_chunk(xx, yy, cc, i):
        return nodes.at[pl.ds(group(xx, yy, cc) * 2 + i, 1)]

    x_peer = [(group((x + d) % 4, y, c), t) for d in range(4)]
    y_peer = [(group(x, (y + d) % 4, c), t) for d in range(4)]
    sibling = (group(x, y, 1 - c), t)
    z_peer = [(g, (t + d) % 8) for d in range(8)]
    everyone = x_peer[1:] + y_peer[1:] + [sibling] + z_peer[1:]

    barrier = pltpu.get_barrier_semaphore()
    for peer in everyone:
        pl.semaphore_signal(barrier, inc=1, device_id=peer, device_id_type=MESH)

    locals_ = []
    for k, (src, dst) in enumerate(
        ((hid, v_hid), (gain, v_gain), (wq, v_wq), (wkv, v_wkv), (private, v_priv), (wo, v_wo),
         (prefix, chunk(x, y, c)))
    ):
        copy = pltpu.make_async_copy(src, dst, l_sem.at[k])
        copy.start()
        locals_.append(copy)

    pl.semaphore_wait(barrier, len(everyone))

    sends = []

    def send(src, dst, ssem, rsem, peer):
        copy = pltpu.make_async_remote_copy(
            src_ref=src, dst_ref=dst, send_sem=ssem, recv_sem=rsem, device_id=peer, device_id_type=MESH
        )
        copy.start()
        sends.append(copy)

    def arrived(ref, sem):
        pltpu.make_async_copy(ref, ref, sem).wait()

    own = chunk(x, y, c)
    for d in (1, 3, 2):
        send(prefix, own, a_send.at[0, d], a_recv.at[0, d], x_peer[d])
        send(prefix, own, a_send.at[1, d], a_recv.at[1, d], y_peer[d])
    send(prefix, own, s_send.at[0, 0], s_recv.at[0, 0], sibling)

    mids = [reqnode[g * REQ + r] for r in range(REQ)]
    root = parent[mids[0]]
    root_length = nlen[root]
    row16 = lax.broadcasted_iota(jnp.int32, (REQ, 128), 0)
    lane16 = lax.broadcasted_iota(jnp.int32, (REQ, 128), 1)
    private_length = jnp.zeros((REQ, 128), jnp.int32)
    mid_length = jnp.zeros((REQ, 128), jnp.int32)
    for r in range(REQ):
        private_length = jnp.where(row16 == r, plen[r], private_length)
        mid_length = jnp.where(row16 == r, nlen[mids[r]], mid_length)
    tables = rope_tables((private_length + mid_length + root_length).astype(F32))

    locals_[0].wait()
    locals_[1].wait()
    floats = v_hid[...].astype(F32)
    spread = jnp.mean(floats * floats, axis=-1, keepdims=True)
    normed = (floats * lax.rsqrt(spread + 1e-05) * v_gain[...].astype(F32)).astype(BF16)
    locals_[2].wait()
    query = dot(normed, v_wq[...])
    for half in range(2):
        piece = rope(query[:, half * 128 : half * 128 + 128], tables).astype(BF16)
        q_all[t, :, half * 128 : half * 128 + 128] = piece * jnp.asarray(HEAD_DIM**-0.5, BF16)
    for d in (4, 3, 5, 2, 6, 1, 7):
        send(q_all.at[t], q_all.at[t], z_send.at[0, d], z_recv.at[0, d], z_peer[d])

    locals_[3].wait()
    keyval = dot(normed, v_wkv[...])
    doubled = jnp.concatenate([keyval, keyval], axis=1)
    keyval = jnp.where(t < KV_HEADS, rope(doubled, tables), doubled).astype(BF16)
    out_kv[...] = keyval[:, :HEAD_DIM]
    kv_send[...] = keyval
    kind = t // KV_HEADS
    for j in range(2):
        target = (t % KV_HEADS) * 2 + j

        @pl.when(target != t)
        def _():
            pltpu.make_async_remote_copy(
                src_ref=kv_send, dst_ref=kv_recv.at[kind], send_sem=kv_ss.at[j],
                recv_sem=kv_rs.at[kind], device_id=(g, target), device_id_type=MESH,
            ).start()

        @pl.when(target == t)
        def _():
            kv_recv[kind] = kv_send[...]

    for d in range(1, 8):
        arrived(q_all.at[(t + 8 - d) % 8], z_recv.at[0, d])
    lane256 = lax.broadcasted_iota(jnp.int32, (REQ, KW), 1)
    pieces = []
    for h in range(HEADS):
        j, k = h % 4, h // 8
        slab = q_all[h // 4].astype(F32)
        shift = ((k - j) * HEAD_DIM) % KW
        if shift:
            slab = pltpu.roll(slab, shift, 1)
        pieces.append(jnp.where(lane256 // HEAD_DIM == k, slab, 0.0).astype(BF16))
    blocked = jnp.concatenate(pieces, axis=0)

    for d in (1, 3, 2):
        arrived(chunk((x + 4 - d) % 4, y, c), a_recv.at[0, d])
        part = half_chunk((x + 4 - d) % 4, y, c, 0)
        for e in (1, 3, 2):
            send(part, part, d_send.at[0, d, e], d_recv.at[0, d, e], y_peer[e])
        arrived(chunk(x, (y + 4 - d) % 4, c), a_recv.at[1, d])
        part = half_chunk(x, (y + 4 - d) % 4, c, 1)
        for e in (1, 3, 2):
            send(part, part, d_send.at[1, e, d], d_recv.at[1, e, d], x_peer[e])
    for d in (1, 3, 2):
        block = chunk((x + 4 - d) % 4, y, c)
        send(block, block, s_send.at[d, 0], s_recv.at[d, 0], sibling)
        block = chunk(x, (y + 4 - d) % 4, c)
        send(block, block, s_send.at[0, d], s_recv.at[0, d], sibling)

    lane3 = lax.broadcasted_iota(jnp.int32, (1, REQ, 128), 2)
    row3 = lax.broadcasted_iota(jnp.int32, (1, REQ, 128), 1)
    slot3 = lane3 % SLOTS + t * SLOTS
    own_half = lane3 // SLOTS == row3 % 2
    shape3 = (HEADS, REQ, 128)

    def pair_mask(pair, half):
        return (row3 // 2 == pair) & half

    def compact(key_quad, half, so_far):
        for q in range(4):
            wide = dot_t(blocked, key_quad(q))
            for e in range(2):
                block = wide[:, e * 128 : e * 128 + 128].reshape(shape3)
                so_far = jnp.where(pair_mask(q * 2 + e, half), block, so_far)
        return so_far

    def weigh(weights, value_quad, half):
        total = None
        for q in range(4):
            wide = jnp.concatenate(
                [
                    jnp.where(pair_mask(q * 2 + e, half), weights, 0.0).astype(BF16).reshape(ROWS, 128)
                    for e in range(2)
                ],
                axis=1,
            )
            term = dot(wide, value_quad(q))
            total = term if total is None else total + term
        return total

    def softmax_part(scores, valid):
        scores = jnp.where(valid, scores, LOW)
        maxima = jnp.max(scores, axis=-1, keepdims=True)
        weights = jnp.where(valid, jnp.exp(scores - maxima), 0.0)
        return weights, maxima, jnp.sum(weights, axis=-1, keepdims=True)

    locals_[4].wait()

    def own_rows(q, lanes):
        return v_priv[q * 4 : q * 4 + 4, :, lanes].reshape(4 * SLOTS, KW)

    keys, values = pl.ds(0, KW), pl.ds(KW, KW)
    scores = compact(lambda q: own_rows(q, keys), own_half, jnp.zeros(shape3, F32))
    valid = own_half & (slot3 < private_length.reshape(1, REQ, 128))
    weights, own_max, own_total = softmax_part(scores, valid)
    own_sum = weigh(weights, lambda q: own_rows(q, values), own_half)

    for d in (1, 3, 2):
        for e in (1, 3, 2):
            xx, yy = (x + 4 - d) % 4, (y + 4 - e) % 4
            arrived(half_chunk(xx, yy, c, 0), d_recv.at[0, d, e])
            arrived(half_chunk(xx, yy, c, 1), d_recv.at[1, d, e])
            block = chunk(xx, yy, c)
            send(block, block, s_send.at[d, e], s_recv.at[d, e], sibling)
    locals_[6].wait()
    for d in range(4):
        for e in range(4):
            arrived(chunk((x + 4 - d) % 4, (y + 4 - e) % 4, 1 - c), s_recv.at[d, e])

    def node_rows(q, lanes):
        order = (q * 4 + 1, q * 4, q * 4 + 3, q * 4 + 2)
        return jnp.concatenate([nodes[mids[r], :, lanes] for r in order], axis=0)

    root_keys = nodes[root, :, keys]
    root_values = nodes[root, :, values]
    root_scores = dot_t(blocked, jnp.concatenate([root_keys, root_keys], axis=0)).reshape(shape3)
    node_half = jnp.logical_not(own_half)
    scores = compact(lambda q: node_rows(q, keys), node_half, root_scores)
    limit = jnp.where(node_half, mid_length.reshape(1, REQ, 128), root_length)
    weights, tree_max, tree_total = softmax_part(scores, slot3 < limit)
    tree_sum = weigh(weights, lambda q: node_rows(q, values), node_half)
    tree_sum = tree_sum + dot(
        jnp.where(own_half, weights, 0.0).astype(BF16).reshape(ROWS, 128),
        jnp.concatenate([root_values, root_values], axis=0),
    )

    upper = jnp.maximum(own_max, tree_max)
    own_scale, tree_scale = jnp.exp(own_max - upper), jnp.exp(tree_max - upper)
    total = own_total * own_scale + tree_total * tree_scale
    narrow = []
    for k in range(KV_HEADS):
        rows, lanes = slice(128 * k, 128 * k + 128), slice(128 * (k // 2), 128 * (k // 2) + 128)
        piece = (
            own_sum[rows, lanes].reshape(8, REQ, 128) * own_scale[8 * k : 8 * k + 8]
            + tree_sum[rows, lanes].reshape(8, REQ, 128) * tree_scale[8 * k : 8 * k + 8]
        ).reshape(128, 128)
        narrow.append(pltpu.roll(piece, HEAD_DIM, 1) if k % 2 else piece)
    packed = jnp.concatenate(narrow, axis=0).reshape(shape3)
    for at, part in enumerate(three_parts(upper) + three_parts(total)):
        packed = jnp.where(lane3 == HEAD_DIM + at, part, packed)
    part_send[...] = packed.astype(BF16).reshape(8, 4 * REQ, 128)
    for d in (4, 3, 5, 2, 6, 1, 7):
        to = (t + d) % 8
        send(part_send.at[to], part_recv.at[t], z_send.at[1, d], z_recv.at[1, d], z_peer[d])

    @pl.when(t // 2 != t)
    def _():
        arrived(kv_recv.at[0], kv_rs.at[0])

    @pl.when(KV_HEADS + t // 2 != t)
    def _():
        arrived(kv_recv.at[1], kv_rs.at[1])

    queries = q_all[t].astype(F32)
    token_key = kv_recv[0].astype(F32)[:, :HEAD_DIM]
    token_value = kv_recv[1].astype(F32)[:, :HEAD_DIM]
    token_score = jnp.concatenate(
        [
            jnp.sum(queries[:, j * HEAD_DIM : (j + 1) * HEAD_DIM] * token_key, axis=-1, keepdims=True)
            for j in range(4)
        ],
        axis=0,
    )
    token_rows = jnp.concatenate([token_value] * 4, axis=0)

    part_recv[t] = part_send[t]
    for d in range(1, 8):
        arrived(part_recv.at[(t + 8 - d) % 8], z_recv.at[1, d])
    parts = [part_recv[s].astype(F32) for s in range(8)]

    def column(part, at):
        first = HEAD_DIM + at
        return part[:, first : first + 1] + part[:, first + 1 : first + 2] + part[:, first + 2 : first + 3]

    maxima = [column(part, 0) for part in parts]
    upper = token_score
    for entry in maxima:
        upper = jnp.maximum(upper, entry)
    fresh = jnp.exp(token_score - upper)
    total = fresh
    summed = fresh.astype(BF16).astype(F32) * token_rows
    for part, entry in zip(parts, maxima):
        factor = jnp.exp(entry - upper)
        total = total + column(part, 3) * factor
        summed = summed + part[:, :HEAD_DIM] * factor
    attention = (summed / total).astype(BF16)
    attention = jnp.concatenate([attention[j * REQ : (j + 1) * REQ] for j in range(4)], axis=1)

    locals_[5].wait()
    projected = dot(attention, v_wo[...])
    for s in range(8):
        rs_send[s] = projected[:, s * 256 : s * 256 + 256].astype(BF16)
    for d in (4, 3, 5, 2, 6, 1, 7):
        to = (t + d) % 8
        send(rs_send.at[to], rs_recv.at[t], z_send.at[2, d], z_recv.at[2, d], z_peer[d])
    rs_recv[t] = rs_send[t]
    for d in range(1, 8):
        arrived(rs_recv.at[(t + 8 - d) % 8], z_recv.at[2, d])
    result = v_hid[:, pl.ds(pl.multiple_of(t * 256, 256), 256)].astype(F32)
    for s in range(8):
        result = result + rs_recv[s].astype(F32)
    out_h[...] = result.astype(BF16)

    for copy in sends:
        copy.wait_send()
    for j in range(2):
        target = (t % KV_HEADS) * 2 + j

        @pl.when(target != t)
        def _():
            pltpu.make_async_copy(kv_send, kv_send, kv_ss.at[j]).wait()


def on_device(
    hidden_in, norm_gain, w_query, w_keyval, w_output, prefix_cache, private_cache,
    node_parent, node_length, request_node, private_length,
):
    anywhere = pl.BlockSpec(memory_space=pl.ANY)
    scalars = pl.BlockSpec(memory_space=pltpu.SMEM)
    vector = pl.BlockSpec(memory_space=pltpu.VMEM)
    dma = pltpu.SemaphoreType.DMA
    return pl.pallas_call(
        kernel,
        out_shape=(
            jax.ShapeDtypeStruct((REQ, 256), BF16),
            jax.ShapeDtypeStruct((REQ, HEAD_DIM), BF16),
        ),
        in_specs=[anywhere] * 7 + [scalars] * 4,
        out_specs=(vector, vector),
        scratch_shapes=[
            pltpu.VMEM((REQ, 2048), BF16),
            pltpu.VMEM((1, 2048), BF16),
            pltpu.VMEM((2048, 256), BF16),
            pltpu.VMEM((2048, 64), BF16),
            pltpu.VMEM((256, 2048), BF16),
            pltpu.VMEM((REQ, SLOTS, 512), BF16),
            pltpu.VMEM((64, SLOTS, 512), BF16),
            pltpu.VMEM((8, REQ, 256), BF16),
            pltpu.VMEM((REQ, 128), BF16),
            pltpu.VMEM((2, REQ, 128), BF16),
            pltpu.VMEM((8, 4 * REQ, 128), BF16),
            pltpu.VMEM((8, 4 * REQ, 128), BF16),
            pltpu.VMEM((8, REQ, 256), BF16),
            pltpu.VMEM((8, REQ, 256), BF16),
            dma((7,)),
            dma((2, 4)),
            dma((2, 4)),
            dma((2, 4, 4)),
            dma((2, 4, 4)),
            dma((4, 4)),
            dma((4, 4)),
            dma((3, 8)),
            dma((3, 8)),
            dma((2,)),
            dma((2,)),
        ],
        compiler_params=pltpu.CompilerParams(
            collective_id=0, has_side_effects=True, vmem_limit_bytes=48 * 1024 * 1024
        ),
    )(
        hidden_in, norm_gain.reshape(1, 2048), w_query, w_keyval, w_output, prefix_cache, private_cache,
        node_parent, node_length, request_node, private_length,
    )


def solution(mesh):
    placed = (
        P("grp", None), P(), P(None, "tp"), P(None, "tp"), P("tp", None), P("grp", "tp", None),
        P("grp", "tp", None), P(), P(), P(), P("grp"),
    )
    return jax.shard_map(
        on_device, mesh=mesh, in_specs=placed, out_specs=(P("grp", "tp"), P("grp", "tp")), check_vma=False
    )
```

time: 478 us -> 48.8 us (0.10); the launches traced: 471 us -> 48.6 us
  waiting for transfers between devices: 159 us -> 0 us
  other arithmetic: 137 us -> 0 us
  blocking collectives: 104 us -> 0 us
  Pallas kernels: 0 us -> 40.9 us
  local copies, waits for them, and re-layouts: 44.5 us -> 6.91 us
  between operations: 15.1 us -> 0.74 us
  matrix products: 11.6 us -> 0 us
    unnamed x4 -> x0, waiting for transfers between devices: 113 us -> none
    all_gather x5 -> x0, blocking collectives: 104 us -> none  [the longest x3 60 us: combined_all(): lax.all_gather(part.astype(kind), axis)]
    scatter-add x6 -> x0, other arithmetic: 70.5 us -> none  [the longest x2 44 us: on_device(): sum_rows.at[picked, level_slot]]
    reduce_scatter x1 -> x0, waiting for transfers between devices: 45.6 us -> none  [on_device(): lax.psum_scatter(projected.astype(jnp.bfloat16), 'tp', scatter_dimension=...]
    reduce_sum x6 -> x0, other arithmetic: 44.4 us -> none  [the longest x2 42.6 us: on_device(): filled = jnp.arange(per_tenant) < jnp.sum(member.astype(jnp.int32))]
    pallas_call x0 -> x1, Pallas kernels: none -> 40.9 us  [on_device(): pl.pallas_call(kernel, out_shape=(jax.ShapeDtypeStruct((REQ, 256), BF16),...]
    gather x9 -> x0, local copies, waits for them, and re-layouts: 17.8 us -> none  [the longest x4 7.82 us: on_device(): node_parent[request_node] == node_id]
    dot_general x10 -> x0, matrix products: 11.6 us -> none  [the longest x2 3.68 us: softmax_part(): jnp.einsum('nkgl,lkd->nkgd', rounded, value_rows, preferred_element_type=...]
  transfers between devices with their start and end apart: 3 -> 0, of which waited for: 2 -> 0; matrix products, arithmetic and copies ran while one was open for 15% -> 0% of each run, Pallas kernels for 0% -> 0%
where the time goes in v1:
time: 48.8 us; the launch traced here: 48.6 us
  Pallas kernels  40.9 us (84%)
  local copies, waits for them, and re-layouts  6.91 us (14%)
  between operations  0.74 us (2%)
    pallas_call x1, Pallas kernels, on_device(): pl.pallas_call(kernel, out_shape=(jax.ShapeDtypeStruct((REQ, 256), BF16),...  40.9 us
    unnamed x21, local copies, waits for them, and re-layouts  6.21 us

profile of v1, /device:TPU:1, one launch (start us, length us, event | category | flops | bytes accessed | tf_op | source)
XLA Modules:
  0.0 48.6 jit_solution(13986917518502698335)
XLA Ops:
  0.6 0.7 %reshape.7.gain = bf16[1,2048]{1,0:T(2,128)(2,1)S(1)} reshape(bf16[2048]{0:T(1024)(128)(2,1)} %param.12) | data formatting | bytes 8192 | tf_op jit(solution)/shard_map/reshape | solution.py:400
  1.3 0.0 copy-start.3
  1.3 0.0 copy-start.4
  1.3 0.0 copy-start.5
  1.3 0.0 copy-start.6
  1.4 0.0 copy-start.7
  1.4 0.0 copy-start.8
  1.4 1.3 %copy.13.wkv = bf16[2048,64]{1,0:T(8,128)(2,1)S(1)} copy(bf16[2048,64]{0,1:T(8,128)(2,1)} %param.14) | data formatting | bytes 524288 | tf_op args[3]
  2.7 0.0 copy-done.3
  2.7 0.0 copy-done.4
  2.7 0.0 copy-done.5
  2.7 0.0 copy-done.6
  2.7 0.0 copy-done.7
  2.8 0.0 copy-done.8
  2.8 0.0 copy-start
  2.8 1.2 %copy-done = bf16[2048,256]{1,0:T(8,128)(2,1)S(1)} copy-done((bf16[2048,256]{1,0:T(8,128)(2,1)S(1)}, bf16[2048,256]{1,0:T(8,128)(2,1)}, u32[]{:S(2)}) %copy-start) | copy-done | bytes 1048600
  4.0 0.0 copy-start.1
  4.0 1.2 %copy-done.1 = bf16[256,2048]{1,0:T(8,128)(2,1)S(1)} copy-done((bf16[256,2048]{1,0:T(8,128)(2,1)S(1)}, bf16[256,2048]{1,0:T(8,128)(2,1)}, u32[]{:S(2)}) %copy-start.1) | copy-done | bytes 1048600
  5.2 0.0 copy-start.2
  5.2 1.2 %copy-done.2 = bf16[16,64,512]{2,1,0:T(8,128)(2,1)S(1)} copy-done((bf16[16,64,512]{2,1,0:T(8,128)(2,1)S(1)}, bf16[16,64,512]{2,1,0:T(8,128)(2,1)}, u32[]{:S(2)}) %copy-start.2) | copy-done | bytes 1048600
  6.4 40.9 %shard_map.122 = (bf16[16,256]{1,0:T(8,128)(2,1)S(1)}, bf16[16,64]{1,0:T(8,128)(2,1)S(1)}) custom-call(bf16[16,2048]{1,0:T(8,128)(2,1)S(1)} %copy-done.4, bf16[1,2048]{1,0:T(2,128)(2,1)S(1)} %reshape.7.gain, bf16[2048,256]{1,0:T(8,128)(2,1)S(1)} %copy-done, bf16[2048,64]{1,0:T(8,128)(2,1)S(1)} %copy.13.wkv, bf16[256,2048]{1,0:T(8,128)(2,1)S(1)} %copy-done.1, ...), custom_call_target="tpu_custom_call" | custom-call | tf_op jit(solution)/shard_map/pallas_call | solution.py:361
  47.4 0.6 %copy.16 = bf16[16,256]{1,0:T(8,128)(2,1)} copy(bf16[16,256]{1,0:T(8,128)(2,1)S(1)} %get-tuple-element.4) | data formatting | bytes 16384
  48.0 0.6 %copy.17 = bf16[16,64]{1,0:T(8,128)(2,1)} copy(bf16[16,64]{1,0:T(8,128)(2,1)S(1)} %get-tuple-element.5) | data formatting | bytes 4096
Async XLA Ops:
  1.3 1.4 %copy-start.3 = (bf16[2,64,512]{2,1,0:T(8,128)(2,1)S(1)}, bf16[2,64,512]{2,1,0:T(8,128)(2,1)}, u32[]{:S(2)}) copy-start(bf16[2,64,512]{2,1,0:T(8,128)(2,1)} %prefix.1) | copy-start | bytes 393220
  1.3 1.4 %copy-start.4 = (bf16[16,2048]{1,0:T(8,128)(2,1)S(1)}, bf16[16,2048]{1,0:T(8,128)(2,1)}, u32[]{:S(2)}) copy-start(bf16[16,2048]{1,0:T(8,128)(2,1)} %hid.1) | copy-start | bytes 196612
  1.3 1.4 %copy-start.5 = (s32[512]{0:T(512)S(1)}, s32[512]{0:T(512)}, u32[]{:S(2)}) copy-start(s32[512]{0:T(512)} %reqnode.1) | copy-start | bytes 6148
  1.3 1.4 %copy-start.6 = (s32[64]{0:T(128)S(1)}, s32[64]{0:T(128)}, u32[]{:S(2)}) copy-start(s32[64]{0:T(128)} %parent.1) | copy-start | bytes 772
  1.4 1.4 %copy-start.7 = (s32[64]{0:T(128)S(1)}, s32[64]{0:T(128)}, u32[]{:S(2)}) copy-start(s32[64]{0:T(128)} %nlen.1) | copy-start | bytes 772
  1.4 1.4 %copy-start.8 = (s32[16]{0:T(128)S(1)}, s32[16]{0:T(128)}, u32[]{:S(2)}) copy-start(s32[16]{0:T(128)} %plen.1) | copy-start | bytes 196
  2.8 1.2 %copy-start = (bf16[2048,256]{1,0:T(8,128)(2,1)S(1)}, bf16[2048,256]{1,0:T(8,128)(2,1)}, u32[]{:S(2)}) copy-start(bf16[2048,256]{1,0:T(8,128)(2,1)} %wq.1) | copy-start | bytes 3145732
  4.0 1.2 %copy-start.1 = (bf16[256,2048]{1,0:T(8,128)(2,1)S(1)}, bf16[256,2048]{1,0:T(8,128)(2,1)}, u32[]{:S(2)}) copy-start(bf16[256,2048]{1,0:T(8,128)(2,1)} %wo.1) | copy-start | bytes 3145732
  5.2 1.2 %copy-start.2 = (bf16[16,64,512]{2,1,0:T(8,128)(2,1)S(1)}, bf16[16,64,512]{2,1,0:T(8,128)(2,1)}, u32[]{:S(2)}) copy-start(bf16[16,64,512]{2,1,0:T(8,128)(2,1)} %private.1) | copy-start | bytes 3145732

commit v2 on v1

--- a/solution.py
+++ b/solution.py
@@ -58,7 +58,7 @@
     out_h, out_kv,
     v_hid, v_gain, v_wq, v_wkv, v_wo, v_priv, nodes,
     q_all, kv_send, kv_recv, part_send, part_recv, rs_send, rs_recv,
-    l_sem, a_send, a_recv, d_send, d_recv, s_send, s_recv, z_send, z_recv, kv_ss, kv_rs,
+    l_sem, d_send, d_recv, s_send, s_recv, z_send, z_recv, kv_ss, kv_rs,
 ):
     g = lax.axis_index("grp")
     t = lax.axis_index("tp")
@@ -70,14 +70,11 @@
     def chunk(xx, yy, cc):
         return nodes.at[pl.ds(group(xx, yy, cc) * 2, 2)]
 
-    def half_chunk(xx, yy, cc, i):
-        return nodes.at[pl.ds(group(xx, yy, cc) * 2 + i, 1)]
-
-    x_peer = [(group((x + d) % 4, y, c), t) for d in range(4)]
-    y_peer = [(group(x, (y + d) % 4, c), t) for d in range(4)]
+    x_peer = {d: (group((x + 4 + d * (1 - 2 * c)) % 4, y, c), t) for d in (1, 2, -1)}
+    y_peer = {d: (group(x, (y + 4 + d * (1 - 2 * c)) % 4, c), t) for d in (1, 2, -1)}
     sibling = (group(x, y, 1 - c), t)
     z_peer = [(g, (t + d) % 8) for d in range(8)]
-    everyone = x_peer[1:] + y_peer[1:] + [sibling] + z_peer[1:]
+    everyone = list(x_peer.values()) + list(y_peer.values()) + [sibling] + z_peer[1:]
 
     barrier = pltpu.get_barrier_semaphore()
     for peer in everyone:
@@ -92,25 +89,36 @@
         copy.start()
         locals_.append(copy)
 
-    pl.semaphore_wait(barrier, len(everyone))
-
-    sends = []
-
     def send(src, dst, ssem, rsem, peer):
-        copy = pltpu.make_async_remote_copy(
+        pltpu.make_async_remote_copy(
             src_ref=src, dst_ref=dst, send_sem=ssem, recv_sem=rsem, device_id=peer, device_id_type=MESH
-        )
-        copy.start()
-        sends.append(copy)
+        ).start()
 
     def arrived(ref, sem):
         pltpu.make_async_copy(ref, ref, sem).wait()
 
-    own = chunk(x, y, c)
-    for d in (1, 3, 2):
-        send(prefix, own, a_send.at[0, d], a_recv.at[0, d], x_peer[d])
-        send(prefix, own, a_send.at[1, d], a_recv.at[1, d], y_peer[d])
-    send(prefix, own, s_send.at[0, 0], s_recv.at[0, 0], sibling)
+    turn = 1 - 2 * c
+
+    def slab(i, a, b):
+        return nodes.at[pl.ds(group((x + 16 - turn * a) % 4, (y + 16 - turn * b) % 4, c) * 2 + i, 1)]
+
+    def hand_on(i, a, b, *ways):
+        block = slab(i, a, b)
+        for axis, step in ways:
+            if axis == "s":
+                send(block, block, s_send, s_recv, sibling)
+                continue
+            aa, bb = ((a + step) % 4, b) if axis == "x" else (a, (b + step) % 4)
+            peer = (x_peer if axis == "x" else y_peer)[step]
+            send(block, block, d_send, d_recv.at[i, aa, bb], peer)
+
+    def relay(i, a, b, *ways):
+        if i == 1:
+            a, b = b, a
+            ways = [({"x": "y", "y": "x"}[axis], step) for axis, step in ways]
+        if a + b:
+            arrived(slab(i, a, b), d_recv.at[i, a, b])
+        hand_on(i, a, b, *ways, ("s", 0))
 
     mids = [reqnode[g * REQ + r] for r in range(REQ)]
     root = parent[mids[0]]
@@ -128,21 +136,27 @@
     locals_[1].wait()
     floats = v_hid[...].astype(F32)
     spread = jnp.mean(floats * floats, axis=-1, keepdims=True)
-    normed = (floats * lax.rsqrt(spread + 1e-05) * v_gain[...].astype(F32)).astype(BF16)
+    normed = (floats * lax.rsqrt(spread + 1e-05) * v_gain[...].reshape(1, 2048).astype(F32)).astype(BF16)
     locals_[2].wait()
     query = dot(normed, v_wq[...])
     for half in range(2):
         piece = rope(query[:, half * 128 : half * 128 + 128], tables).astype(BF16)
         q_all[t, :, half * 128 : half * 128 + 128] = piece * jnp.asarray(HEAD_DIM**-0.5, BF16)
-    for d in (4, 3, 5, 2, 6, 1, 7):
-        send(q_all.at[t], q_all.at[t], z_send.at[0, d], z_recv.at[0, d], z_peer[d])
-
     locals_[3].wait()
-    keyval = dot(normed, v_wkv[...])
+    keyval = dot_t(normed, v_wkv[...])
     doubled = jnp.concatenate([keyval, keyval], axis=1)
     keyval = jnp.where(t < KV_HEADS, rope(doubled, tables), doubled).astype(BF16)
     out_kv[...] = keyval[:, :HEAD_DIM]
     kv_send[...] = keyval
+    locals_[6].wait()
+    pl.semaphore_wait(barrier, len(everyone))
+    hand_on(0, 0, 0, ("x", 2), ("x", 1), ("x", -1))
+    hand_on(1, 0, 0, ("y", 2), ("y", 1), ("y", -1))
+    for d in (4, 3, 5, 2, 6, 1, 7):
+        send(q_all.at[t], q_all.at[t], z_send.at[0], z_recv.at[0], z_peer[d])
+    hand_on(0, 0, 0, ("y", 1), ("y", -1), ("s", 0))
+    hand_on(1, 0, 0, ("x", 1), ("x", -1), ("s", 0))
+
     kind = t // KV_HEADS
     for j in range(2):
         target = (t % KV_HEADS) * 2 + j
@@ -158,34 +172,42 @@
         def _():
             kv_recv[kind] = kv_send[...]
 
-    for d in range(1, 8):
-        arrived(q_all.at[(t + 8 - d) % 8], z_recv.at[0, d])
+    def relay_first():
+        for a in (1, 3):
+            for i in range(2):
+                relay(i, a, 0, ("y", 1), ("y", -1))
+        for i in range(2):
+            relay(i, 2, 0, ("y", 2), ("y", 1), ("y", -1))
+
+    def relay_second():
+        for i in range(2):
+            relay(i, 0, 1, ("y", 1))
+            relay(i, 0, 3)
+        for i in range(2):
+            relay(i, 1, 1, ("y", 1))
+            relay(i, 3, 3, ("y", -1))
+
+    def relay_last():
+        for where in ((1, 3), (3, 1), (2, 1), (2, 3), (0, 2), (2, 2), (1, 2), (3, 2)):
+            for i in range(2):
+                relay(i, *where)
+        arrived(nodes.at[pl.ds(0, 32)], s_recv)
+
+    relay_first()
+
+    arrived(q_all.at[pl.ds(0, 7)], z_recv.at[0])
     lane256 = lax.broadcasted_iota(jnp.int32, (REQ, KW), 1)
     pieces = []
     for h in range(HEADS):
         j, k = h % 4, h // 8
-        slab = q_all[h // 4].astype(F32)
+        four = q_all[h // 4].astype(F32)
         shift = ((k - j) * HEAD_DIM) % KW
         if shift:
-            slab = pltpu.roll(slab, shift, 1)
-        pieces.append(jnp.where(lane256 // HEAD_DIM == k, slab, 0.0).astype(BF16))
+            four = pltpu.roll(four, shift, 1)
+        pieces.append(jnp.where(lane256 // HEAD_DIM == k, four, 0.0).astype(BF16))
     blocked = jnp.concatenate(pieces, axis=0)
 
-    for d in (1, 3, 2):
-        arrived(chunk((x + 4 - d) % 4, y, c), a_recv.at[0, d])
-        part = half_chunk((x + 4 - d) % 4, y, c, 0)
-        for e in (1, 3, 2):
-            send(part, part, d_send.at[0, d, e], d_recv.at[0, d, e], y_peer[e])
-        arrived(chunk(x, (y + 4 - d) % 4, c), a_recv.at[1, d])
-        part = half_chunk(x, (y + 4 - d) % 4, c, 1)
-        for e in (1, 3, 2):
-            send(part, part, d_send.at[1, e, d], d_recv.at[1, e, d], x_peer[e])
-    for d in (1, 3, 2):
-        block = chunk((x + 4 - d) % 4, y, c)
-        send(block, block, s_send.at[d, 0], s_recv.at[d, 0], sibling)
-        block = chunk(x, (y + 4 - d) % 4, c)
-        send(block, block, s_send.at[0, d], s_recv.at[0, d], sibling)
-
+    relay_second()
     lane3 = lax.broadcasted_iota(jnp.int32, (1, REQ, 128), 2)
     row3 = lax.broadcasted_iota(jnp.int32, (1, REQ, 128), 1)
     slot3 = lane3 % SLOTS + t * SLOTS
@@ -234,17 +256,7 @@
     weights, own_max, own_total = softmax_part(scores, valid)
     own_sum = weigh(weights, lambda q: own_rows(q, values), own_half)
 
-    for d in (1, 3, 2):
-        for e in (1, 3, 2):
-            xx, yy = (x + 4 - d) % 4, (y + 4 - e) % 4
-            arrived(half_chunk(xx, yy, c, 0), d_recv.at[0, d, e])
-            arrived(half_chunk(xx, yy, c, 1), d_recv.at[1, d, e])
-            block = chunk(xx, yy, c)
-            send(block, block, s_send.at[d, e], s_recv.at[d, e], sibling)
-    locals_[6].wait()
-    for d in range(4):
-        for e in range(4):
-            arrived(chunk((x + 4 - d) % 4, (y + 4 - e) % 4, 1 - c), s_recv.at[d, e])
+    relay_last()
 
     def node_rows(q, lanes):
         order = (q * 4 + 1, q * 4, q * 4 + 3, q * 4 + 2)
@@ -280,8 +292,11 @@
     part_send[...] = packed.astype(BF16).reshape(8, 4 * REQ, 128)
     for d in (4, 3, 5, 2, 6, 1, 7):
         to = (t + d) % 8
-        send(part_send.at[to], part_recv.at[t], z_send.at[1, d], z_recv.at[1, d], z_peer[d])
-
+        send(part_send.at[to], part_recv.at[t], z_send.at[1], z_recv.at[1], z_peer[d])
+
+    arrived(nodes.at[pl.ds(0, 30)], d_send)
+    arrived(nodes.at[pl.ds(0, 32)], s_send)
+    arrived(q_all.at[pl.ds(0, 7)], z_send.at[0])
     @pl.when(t // 2 != t)
     def _():
         arrived(kv_recv.at[0], kv_rs.at[0])
@@ -303,8 +318,7 @@
     token_rows = jnp.concatenate([token_value] * 4, axis=0)
 
     part_recv[t] = part_send[t]
-    for d in range(1, 8):
-        arrived(part_recv.at[(t + 8 - d) % 8], z_recv.at[1, d])
+    arrived(part_recv.at[pl.ds(0, 7)], z_recv.at[1])
     parts = [part_recv[s].astype(F32) for s in range(8)]
 
     def column(part, at):
@@ -326,22 +340,22 @@
     attention = jnp.concatenate([attention[j * REQ : (j + 1) * REQ] for j in range(4)], axis=1)
 
     locals_[5].wait()
-    projected = dot(attention, v_wo[...])
-    for s in range(8):
-        rs_send[s] = projected[:, s * 256 : s * 256 + 256].astype(BF16)
-    for d in (4, 3, 5, 2, 6, 1, 7):
+    for d in (4, 3, 5, 2, 6, 1, 7, 0):
         to = (t + d) % 8
-        send(rs_send.at[to], rs_recv.at[t], z_send.at[2, d], z_recv.at[2, d], z_peer[d])
-    rs_recv[t] = rs_send[t]
-    for d in range(1, 8):
-        arrived(rs_recv.at[(t + 8 - d) % 8], z_recv.at[2, d])
+        block = dot(attention, v_wo[:, pl.ds(pl.multiple_of(to * 256, 256), 256)]).astype(BF16)
+        if d:
+            rs_send[to] = block
+            send(rs_send.at[to], rs_recv.at[t], z_send.at[2], z_recv.at[2], z_peer[d])
+        else:
+            rs_recv[t] = block
+    arrived(rs_recv.at[pl.ds(0, 7)], z_recv.at[2])
     result = v_hid[:, pl.ds(pl.multiple_of(t * 256, 256), 256)].astype(F32)
     for s in range(8):
         result = result + rs_recv[s].astype(F32)
     out_h[...] = result.astype(BF16)
 
-    for copy in sends:
-        copy.wait_send()
+    arrived(part_send.at[pl.ds(0, 7)], z_send.at[1])
+    arrived(rs_send.at[pl.ds(0, 7)], z_send.at[2])
     for j in range(2):
         target = (t % KV_HEADS) * 2 + j
 
@@ -354,7 +368,7 @@
     hidden_in, norm_gain, w_query, w_keyval, w_output, prefix_cache, private_cache,
     node_parent, node_length, request_node, private_length,
 ):
-    anywhere = pl.BlockSpec(memory_space=pl.ANY)
+    anywhere = pl.BlockSpec(memory_space=pltpu.HBM)
     scalars = pl.BlockSpec(memory_space=pltpu.SMEM)
     vector = pl.BlockSpec(memory_space=pltpu.VMEM)
     dma = pltpu.SemaphoreType.DMA
@@ -368,9 +382,9 @@
         out_specs=(vector, vector),
         scratch_shapes=[
             pltpu.VMEM((REQ, 2048), BF16),
-            pltpu.VMEM((1, 2048), BF16),
+            pltpu.VMEM((2048,), BF16),
             pltpu.VMEM((2048, 256), BF16),
-            pltpu.VMEM((2048, 64), BF16),
+            pltpu.VMEM((64, 2048), BF16),
             pltpu.VMEM((256, 2048), BF16),
             pltpu.VMEM((REQ, SLOTS, 512), BF16),
             pltpu.VMEM((64, SLOTS, 512), BF16),
@@ -382,22 +396,20 @@
             pltpu.VMEM((8, REQ, 256), BF16),
             pltpu.VMEM((8, REQ, 256), BF16),
             dma((7,)),
-            dma((2, 4)),
-            dma((2, 4)),
+            dma,
             dma((2, 4, 4)),
-            dma((2, 4, 4)),
-            dma((4, 4)),
-            dma((4, 4)),
-            dma((3, 8)),
-            dma((3, 8)),
+            dma,
+            dma,
+            dma((3,)),
+            dma((3,)),
             dma((2,)),
             dma((2,)),
         ],
         compiler_params=pltpu.CompilerParams(
-            collective_id=0, has_side_effects=True, vmem_limit_bytes=48 * 1024 * 1024
+            collective_id=0, has_side_effects=True, vmem_limit_bytes=63 * 1024 * 1024
         ),
     )(
-        hidden_in, norm_gain.reshape(1, 2048), w_query, w_keyval, w_output, prefix_cache, private_cache,
+        hidden_in, norm_gain, w_query, w_keyval.T, w_output, prefix_cache, private_cache,
         node_parent, node_length, request_node, private_length,
     )
 

time: 48.8 us -> 41.6 us (0.85)
  local copies, waits for them, and re-layouts: 6.91 us -> 1.89 us
  Pallas kernels: 40.9 us -> 38.9 us
    unnamed x21 -> x4, local copies, waits for them, and re-layouts: 6.21 us -> 1.89 us
    pallas_call x1, Pallas kernels: 40.9 us -> 38.9 us  [on_device(): pl.pallas_call(kernel, out_shape=(jax.ShapeDtypeStruct((REQ, 256), BF16),...]
    reshape x1 -> x0, local copies, waits for them, and re-layouts: 0.69 us -> none  [on_device(): norm_gain.reshape(1, 2048)]
where the time goes in v2:
time: 41.6 us; the launch traced here: 41.5 us
  Pallas kernels  38.9 us (94%)
  local copies, waits for them, and re-layouts  1.89 us (5%)
  between operations  0.65 us (2%)
    pallas_call x1, Pallas kernels, on_device(): pl.pallas_call(kernel, out_shape=(jax.ShapeDtypeStruct((REQ, 256), BF16),...  38.9 us
    unnamed x4, local copies, waits for them, and re-layouts  1.89 us

profile of v2, /device:TPU:1, one launch (start us, length us, event | category | flops | bytes accessed | tf_op | source)
XLA Modules:
  0.0 41.5 jit_solution(5897172187843734282)
XLA Ops:
  0.6 38.9 %shard_map.122 = (bf16[16,256]{1,0:T(8,128)(2,1)}, bf16[16,64]{1,0:T(8,128)(2,1)}) custom-call(bf16[16,2048]{1,0:T(8,128)(2,1)} %hid.1, bf16[2048]{0:T(1024)(128)(2,1)} %gain.1, bf16[2048,256]{1,0:T(8,128)(2,1)} %wq.1, bf16[64,2048]{1,0:T(8,128)(2,1)} %bitcast.1, bf16[256,2048]{1,0:T(8,128)(2,1)} %wo.1, bf16[2,64,512]{2,1,0:T(8,128)(2,1)} %prefix.1, ...), custom_call_target="tpu_custom_call" | custom-call | tf_op jit(solution)/shard_map/pallas_call | solution.py:375
  39.6 0.0 copy-start
  39.6 1.3 %copy.15 = bf16[16,256]{1,0:T(8,128)(2,1)} copy(bf16[16,256]{1,0:T(8,128)(2,1)} %get-tuple-element.4) | data formatting | bytes 16384
  40.9 0.0 copy-done
  40.9 0.6 %copy.16 = bf16[16,64]{1,0:T(8,128)(2,1)} copy(bf16[16,64]{1,0:T(8,128)(2,1)S(1)} %copy-done) | data formatting | bytes 4096
Async XLA Ops:
  39.6 1.3 %copy-start = (bf16[16,64]{1,0:T(8,128)(2,1)S(1)}, bf16[16,64]{1,0:T(8,128)(2,1)}, u32[]{:S(2)}) copy-start(bf16[16,64]{1,0:T(8,128)(2,1)} %get-tuple-element.5) | copy-start | bytes 6148

commit v3 on v2

--- a/solution.py
+++ b/solution.py
@@ -103,14 +103,14 @@
         return nodes.at[pl.ds(group((x + 16 - turn * a) % 4, (y + 16 - turn * b) % 4, c) * 2 + i, 1)]
 
     def hand_on(i, a, b, *ways):
-        block = slab(i, a, b)
+        block = prefix.at[pl.ds(i, 1)] if a + b == 0 else slab(i, a, b)
         for axis, step in ways:
             if axis == "s":
-                send(block, block, s_send, s_recv, sibling)
+                send(block, slab(i, a, b), s_send, s_recv, sibling)
                 continue
             aa, bb = ((a + step) % 4, b) if axis == "x" else (a, (b + step) % 4)
             peer = (x_peer if axis == "x" else y_peer)[step]
-            send(block, block, d_send, d_recv.at[i, aa, bb], peer)
+            send(block, slab(i, a, b), d_send, d_recv.at[i, aa, bb], peer)
 
     def relay(i, a, b, *ways):
         if i == 1:
@@ -119,6 +119,12 @@
         if a + b:
             arrived(slab(i, a, b), d_recv.at[i, a, b])
         hand_on(i, a, b, *ways, ("s", 0))
+
+    pl.semaphore_wait(barrier, len(everyone))
+    hand_on(0, 0, 0, ("x", 2), ("x", 1), ("x", -1))
+    hand_on(1, 0, 0, ("y", 2), ("y", 1), ("y", -1))
+    hand_on(0, 0, 0, ("y", 1), ("y", -1), ("s", 0))
+    hand_on(1, 0, 0, ("x", 1), ("x", -1), ("s", 0))
 
     mids = [reqnode[g * REQ + r] for r in range(REQ)]
     root = parent[mids[0]]
@@ -148,15 +154,8 @@
     keyval = jnp.where(t < KV_HEADS, rope(doubled, tables), doubled).astype(BF16)
     out_kv[...] = keyval[:, :HEAD_DIM]
     kv_send[...] = keyval
-    locals_[6].wait()
-    pl.semaphore_wait(barrier, len(everyone))
-    hand_on(0, 0, 0, ("x", 2), ("x", 1), ("x", -1))
-    hand_on(1, 0, 0, ("y", 2), ("y", 1), ("y", -1))
     for d in (4, 3, 5, 2, 6, 1, 7):
         send(q_all.at[t], q_all.at[t], z_send.at[0], z_recv.at[0], z_peer[d])
-    hand_on(0, 0, 0, ("y", 1), ("y", -1), ("s", 0))
-    hand_on(1, 0, 0, ("x", 1), ("x", -1), ("s", 0))
-
     kind = t // KV_HEADS
     for j in range(2):
         target = (t % KV_HEADS) * 2 + j
@@ -257,6 +256,7 @@
     own_sum = weigh(weights, lambda q: own_rows(q, values), own_half)
 
     relay_last()
+    locals_[6].wait()
 
     def node_rows(q, lanes):
         order = (q * 4 + 1, q * 4, q * 4 + 3, q * 4 + 2)
@@ -406,11 +406,16 @@
             dma((2,)),
         ],
         compiler_params=pltpu.CompilerParams(
-            collective_id=0, has_side_effects=True, vmem_limit_bytes=63 * 1024 * 1024
+            collective_id=0, has_side_effects=True, vmem_limit_bytes=40 * 1024 * 1024
         ),
     )(
-        hidden_in, norm_gain, w_query, w_keyval.T, w_output, prefix_cache, private_cache,
-        node_parent, node_length, request_node, private_length,
+        *(
+            pltpu.with_memory_space_constraint(array, pltpu.HBM)
+            for array in (
+                hidden_in, norm_gain, w_query, w_keyval.T, w_output, prefix_cache, private_cache,
+                node_parent, node_length, request_node, private_length,
+            )
+        )
     )
 
 

time: 41.6 us -> 40.5 us (0.974)
  local copies, waits for them, and re-layouts: 1.89 us -> 1.19 us
    unnamed x4 -> x2, local copies, waits for them, and re-layouts: 1.89 us -> 1.19 us
where the time goes in v3:
time: 40.5 us; the launch traced here: 40.4 us
  Pallas kernels  38.6 us (95%)
  local copies, waits for them, and re-layouts  1.19 us (3%)
  between operations  0.64 us (2%)
    pallas_call x1, Pallas kernels, on_device(): pl.pallas_call(kernel, out_shape=(jax.ShapeDtypeStruct((REQ, 256), BF16),...  38.6 us
    unnamed x2, local copies, waits for them, and re-layouts  1.19 us

profile of v3, /device:TPU:1, one launch (start us, length us, event | category | flops | bytes accessed | tf_op | source)
XLA Modules:
  0.0 40.4 jit_solution(1381722751480552324)
XLA Ops:
  0.6 38.6 %shard_map.122 = (bf16[16,256]{1,0:T(8,128)(2,1)S(1)}, bf16[16,64]{1,0:T(8,128)(2,1)S(1)}) custom-call(bf16[16,2048]{1,0:T(8,128)(2,1)} %hid.1, bf16[2048]{0:T(1024)(128)(2,1)} %gain.1, bf16[2048,256]{1,0:T(8,128)(2,1)} %wq.1, bf16[64,2048]{1,0:T(8,128)(2,1)} %bitcast.1, bf16[256,2048]{1,0:T(8,128)(2,1)} %wo.1, bf16[2,64,512]{2,1,0:T(8,128)(2,1)} %prefix.1, ...), custom_call_target="tpu_custom_call" | custom-call | tf_op jit(solution)/shard_map/pallas_call | solution.py:375
  39.2 0.6 %copy.15 = bf16[16,256]{1,0:T(8,128)(2,1)} copy(bf16[16,256]{1,0:T(8,128)(2,1)S(1)} %get-tuple-element.4) | data formatting | bytes 16384
  39.8 0.6 %copy.16 = bf16[16,64]{1,0:T(8,128)(2,1)} copy(bf16[16,64]{1,0:T(8,128)(2,1)S(1)} %get-tuple-element.5) | data formatting | bytes 4096

commit v4 on v3

--- a/solution.py
+++ b/solution.py
@@ -278,18 +278,23 @@
     upper = jnp.maximum(own_max, tree_max)
     own_scale, tree_scale = jnp.exp(own_max - upper), jnp.exp(tree_max - upper)
     total = own_total * own_scale + tree_total * tree_scale
-    narrow = []
-    for k in range(KV_HEADS):
-        rows, lanes = slice(128 * k, 128 * k + 128), slice(128 * (k // 2), 128 * (k // 2) + 128)
-        piece = (
-            own_sum[rows, lanes].reshape(8, REQ, 128) * own_scale[8 * k : 8 * k + 8]
-            + tree_sum[rows, lanes].reshape(8, REQ, 128) * tree_scale[8 * k : 8 * k + 8]
-        ).reshape(128, 128)
-        narrow.append(pltpu.roll(piece, HEAD_DIM, 1) if k % 2 else piece)
-    packed = jnp.concatenate(narrow, axis=0).reshape(shape3)
-    for at, part in enumerate(three_parts(upper) + three_parts(total)):
-        packed = jnp.where(lane3 == HEAD_DIM + at, part, packed)
-    part_send[...] = packed.astype(BF16).reshape(8, 4 * REQ, 128)
+    stats = three_parts(upper) + three_parts(total)
+    low_half = lane16 < HEAD_DIM
+    for p in range(8):
+        for b in range(2):
+            pair = []
+            for e in range(2):
+                h = 4 * p + 2 * b + e
+                k = h // 8
+                rows, lanes = slice(REQ * h, REQ * h + REQ), slice(128 * (k // 2), 128 * (k // 2) + 128)
+                piece = own_sum[rows, lanes] * own_scale[h] + tree_sum[rows, lanes] * tree_scale[h]
+                pair.append(piece if k % 2 == e else pltpu.roll(piece, HEAD_DIM, 1))
+            part_send[p, :, 128 * b : 128 * b + 128] = jnp.where(low_half, *pair).astype(BF16)
+        packed = jnp.zeros((REQ, 128), F32)
+        for j in range(4):
+            for at, part in enumerate(stats):
+                packed = jnp.where(lane16 == 6 * j + at, part[4 * p + j], packed)
+        part_send[p, :, 256:384] = packed.astype(BF16)
     for d in (4, 3, 5, 2, 6, 1, 7):
         to = (t + d) % 8
         send(part_send.at[to], part_recv.at[t], z_send.at[1], z_recv.at[1], z_peer[d])
@@ -306,38 +311,43 @@
         arrived(kv_recv.at[1], kv_rs.at[1])
 
     queries = q_all[t].astype(F32)
-    token_key = kv_recv[0].astype(F32)[:, :HEAD_DIM]
-    token_value = kv_recv[1].astype(F32)[:, :HEAD_DIM]
-    token_score = jnp.concatenate(
-        [
-            jnp.sum(queries[:, j * HEAD_DIM : (j + 1) * HEAD_DIM] * token_key, axis=-1, keepdims=True)
-            for j in range(4)
-        ],
-        axis=0,
-    )
-    token_rows = jnp.concatenate([token_value] * 4, axis=0)
+    token_key = kv_recv[0].astype(F32)
+    token_value = kv_recv[1].astype(F32)
+    token_score = jnp.zeros((REQ, 128), F32)
+    for j in range(4):
+        product = queries[:, j // 2 * 128 : j // 2 * 128 + 128] * token_key
+        product = jnp.where(low_half if j % 2 == 0 else jnp.logical_not(low_half), product, 0.0)
+        token_score = jnp.where(lane16 == 6 * j, jnp.sum(product, axis=-1, keepdims=True), token_score)
 
     part_recv[t] = part_send[t]
     arrived(part_recv.at[pl.ds(0, 7)], z_recv.at[1])
-    parts = [part_recv[s].astype(F32) for s in range(8)]
-
-    def column(part, at):
-        first = HEAD_DIM + at
-        return part[:, first : first + 1] + part[:, first + 1 : first + 2] + part[:, first + 2 : first + 3]
-
-    maxima = [column(part, 0) for part in parts]
+
+    maxima, totals = [], []
+    for s in range(8):
+        stat = part_recv[s, :, 256:384].astype(F32)
+        stat = stat + pltpu.roll(stat, 127, 1) + pltpu.roll(stat, 126, 1)
+        maxima.append(stat)
+        totals.append(pltpu.roll(stat, 125, 1))
     upper = token_score
     for entry in maxima:
         upper = jnp.maximum(upper, entry)
     fresh = jnp.exp(token_score - upper)
     total = fresh
-    summed = fresh.astype(BF16).astype(F32) * token_rows
-    for part, entry in zip(parts, maxima):
-        factor = jnp.exp(entry - upper)
-        total = total + column(part, 3) * factor
-        summed = summed + part[:, :HEAD_DIM] * factor
-    attention = (summed / total).astype(BF16)
-    attention = jnp.concatenate([attention[j * REQ : (j + 1) * REQ] for j in range(4)], axis=1)
+    factors = []
+    for entry, share in zip(maxima, totals):
+        factors.append(jnp.exp(entry - upper))
+        total = total + share * factors[-1]
+
+    def widen(value, b):
+        return jnp.where(low_half, value[:, 12 * b : 12 * b + 1], value[:, 12 * b + 6 : 12 * b + 7])
+
+    halves = []
+    for b in range(2):
+        summed = widen(fresh.astype(BF16).astype(F32), b) * token_value
+        for s in range(8):
+            summed = summed + part_recv[s, :, 128 * b : 128 * b + 128].astype(F32) * widen(factors[s], b)
+        halves.append((summed / widen(total, b)).astype(BF16))
+    attention = jnp.concatenate(halves, axis=1)
 
     locals_[5].wait()
     for d in (4, 3, 5, 2, 6, 1, 7, 0):
@@ -391,8 +401,8 @@
             pltpu.VMEM((8, REQ, 256), BF16),
             pltpu.VMEM((REQ, 128), BF16),
             pltpu.VMEM((2, REQ, 128), BF16),
-            pltpu.VMEM((8, 4 * REQ, 128), BF16),
-            pltpu.VMEM((8, 4 * REQ, 128), BF16),
+            pltpu.VMEM((8, REQ, 384), BF16),
+            pltpu.VMEM((8, REQ, 384), BF16),
             pltpu.VMEM((8, REQ, 256), BF16),
             pltpu.VMEM((8, REQ, 256), BF16),
             dma((7,)),

time: 40.5 us -> 39.9 us (0.985)
  Pallas kernels: 38.6 us -> 37.9 us
    pallas_call x1, Pallas kernels: 38.6 us -> 37.9 us  [on_device(): pl.pallas_call(kernel, out_shape=(jax.ShapeDtypeStruct((REQ, 256), BF16),...]
where the time goes in v4:
time: 39.9 us; the launch traced here: 39.8 us
  Pallas kernels  37.9 us (95%)
  local copies, waits for them, and re-layouts  1.19 us (3%)
  between operations  0.64 us (2%)
    pallas_call x1, Pallas kernels, on_device(): pl.pallas_call(kernel, out_shape=(jax.ShapeDtypeStruct((REQ, 256), BF16),...  37.9 us
    unnamed x2, local copies, waits for them, and re-layouts  1.19 us

profile of v4, /device:TPU:1, one launch (start us, length us, event | category | flops | bytes accessed | tf_op | source)
XLA Modules:
  0.0 39.8 jit_solution(9750331201830920164)
XLA Ops:
  0.6 37.9 %shard_map.122 = (bf16[16,256]{1,0:T(8,128)(2,1)S(1)}, bf16[16,64]{1,0:T(8,128)(2,1)S(1)}) custom-call(bf16[16,2048]{1,0:T(8,128)(2,1)} %hid.1, bf16[2048]{0:T(1024)(128)(2,1)} %gain.1, bf16[2048,256]{1,0:T(8,128)(2,1)} %wq.1, bf16[64,2048]{1,0:T(8,128)(2,1)} %bitcast.1, bf16[256,2048]{1,0:T(8,128)(2,1)} %wo.1, bf16[2,64,512]{2,1,0:T(8,128)(2,1)} %prefix.1, ...), custom_call_target="tpu_custom_call" | custom-call | tf_op jit(solution)/shard_map/pallas_call | solution.py:385
  38.6 0.6 %copy.15 = bf16[16,256]{1,0:T(8,128)(2,1)} copy(bf16[16,256]{1,0:T(8,128)(2,1)S(1)} %get-tuple-element.4) | data formatting | bytes 16384
  39.2 0.6 %copy.16 = bf16[16,64]{1,0:T(8,128)(2,1)} copy(bf16[16,64]{1,0:T(8,128)(2,1)S(1)} %get-tuple-element.5) | data formatting | bytes 4096

commit v5 on v4

--- a/solution.py
+++ b/solution.py
@@ -121,8 +121,10 @@
         hand_on(i, a, b, *ways, ("s", 0))
 
     pl.semaphore_wait(barrier, len(everyone))
-    hand_on(0, 0, 0, ("x", 2), ("x", 1), ("x", -1))
-    hand_on(1, 0, 0, ("y", 2), ("y", 1), ("y", -1))
+    hand_on(0, 0, 0, ("x", 1), ("x", -1))
+    hand_on(1, 0, 0, ("y", 1), ("y", -1))
+    hand_on(0, 0, 0, ("x", 2))
+    hand_on(1, 0, 0, ("y", 2))
     hand_on(0, 0, 0, ("y", 1), ("y", -1), ("s", 0))
     hand_on(1, 0, 0, ("x", 1), ("x", -1), ("s", 0))
 

time: 39.9 us -> 39.4 us (0.987)
  Pallas kernels: 37.9 us -> 37.5 us
    pallas_call x1, Pallas kernels: 37.9 us -> 37.5 us  [on_device(): pl.pallas_call(kernel, out_shape=(jax.ShapeDtypeStruct((REQ, 256), BF16),...]
where the time goes in v5:
time: 39.4 us; the launch traced here: 39.3 us
  Pallas kernels  37.5 us (95%)
  local copies, waits for them, and re-layouts  1.19 us (3%)
  between operations  0.64 us (2%)
    pallas_call x1, Pallas kernels, on_device(): pl.pallas_call(kernel, out_shape=(jax.ShapeDtypeStruct((REQ, 256), BF16),...  37.5 us
    unnamed x2, local copies, waits for them, and re-layouts  1.19 us

profile of v5, /device:TPU:1, one launch (start us, length us, event | category | flops | bytes accessed | tf_op | source)
XLA Modules:
  0.0 39.3 jit_solution(13080257032635167950)
XLA Ops:
  0.6 37.5 %shard_map.122 = (bf16[16,256]{1,0:T(8,128)(2,1)S(1)}, bf16[16,64]{1,0:T(8,128)(2,1)S(1)}) custom-call(bf16[16,2048]{1,0:T(8,128)(2,1)} %hid.1, bf16[2048]{0:T(1024)(128)(2,1)} %gain.1, bf16[2048,256]{1,0:T(8,128)(2,1)} %wq.1, bf16[64,2048]{1,0:T(8,128)(2,1)} %bitcast.1, bf16[256,2048]{1,0:T(8,128)(2,1)} %wo.1, bf16[2,64,512]{2,1,0:T(8,128)(2,1)} %prefix.1, ...), custom_call_target="tpu_custom_call" | custom-call | tf_op jit(solution)/shard_map/pallas_call | solution.py:387
  38.1 0.6 %copy.15 = bf16[16,256]{1,0:T(8,128)(2,1)} copy(bf16[16,256]{1,0:T(8,128)(2,1)S(1)} %get-tuple-element.4) | data formatting | bytes 16384
  38.7 0.6 %copy.16 = bf16[16,64]{1,0:T(8,128)(2,1)} copy(bf16[16,64]{1,0:T(8,128)(2,1)S(1)} %get-tuple-element.5) | data formatting | bytes 4096

commit v6 on v5

--- a/solution.py
+++ b/solution.py
@@ -54,9 +54,9 @@
 
 
 def kernel(
-    hid, gain, wq, wkv, wo, prefix, private, parent, nlen, reqnode, plen,
+    hid, gain, wq, wkv, wo, prefix, private, parent_in, nlen_in, reqnode_in, plen_in,
     out_h, out_kv,
-    v_hid, v_gain, v_wq, v_wkv, v_wo, v_priv, nodes,
+    v_hid, v_gain, v_wq, v_wkv, v_wo, v_priv, parent, nlen, reqnode, plen, nodes,
     q_all, kv_send, kv_recv, part_send, part_recv, rs_send, rs_recv,
     l_sem, d_send, d_recv, s_send, s_recv, z_send, z_recv, kv_ss, kv_rs,
 ):
@@ -83,7 +83,7 @@
     locals_ = []
     for k, (src, dst) in enumerate(
         ((hid, v_hid), (gain, v_gain), (wq, v_wq), (wkv, v_wkv), (private, v_priv), (wo, v_wo),
-         (prefix, chunk(x, y, c)))
+         (prefix, chunk(x, y, c)), (parent_in, parent), (nlen_in, nlen), (reqnode_in, reqnode), (plen_in, plen))
     ):
         copy = pltpu.make_async_copy(src, dst, l_sem.at[k])
         copy.start()
@@ -128,6 +128,8 @@
     hand_on(0, 0, 0, ("y", 1), ("y", -1), ("s", 0))
     hand_on(1, 0, 0, ("x", 1), ("x", -1), ("s", 0))
 
+    for k in range(7, 11):
+        locals_[k].wait()
     mids = [reqnode[g * REQ + r] for r in range(REQ)]
     root = parent[mids[0]]
     root_length = nlen[root]
@@ -381,7 +383,6 @@
     node_parent, node_length, request_node, private_length,
 ):
     anywhere = pl.BlockSpec(memory_space=pltpu.HBM)
-    scalars = pl.BlockSpec(memory_space=pltpu.SMEM)
     vector = pl.BlockSpec(memory_space=pltpu.VMEM)
     dma = pltpu.SemaphoreType.DMA
     return pl.pallas_call(
@@ -390,7 +391,7 @@
             jax.ShapeDtypeStruct((REQ, 256), BF16),
             jax.ShapeDtypeStruct((REQ, HEAD_DIM), BF16),
         ),
-        in_specs=[anywhere] * 7 + [scalars] * 4,
+        in_specs=[anywhere] * 11,
         out_specs=(vector, vector),
         scratch_shapes=[
             pltpu.VMEM((REQ, 2048), BF16),
@@ -399,6 +400,10 @@
             pltpu.VMEM((64, 2048), BF16),
             pltpu.VMEM((256, 2048), BF16),
             pltpu.VMEM((REQ, SLOTS, 512), BF16),
+            pltpu.SMEM((64,), jnp.int32),
+            pltpu.SMEM((64,), jnp.int32),
+            pltpu.SMEM((512,), jnp.int32),
+            pltpu.SMEM((REQ,), jnp.int32),
             pltpu.VMEM((64, SLOTS, 512), BF16),
             pltpu.VMEM((8, REQ, 256), BF16),
             pltpu.VMEM((REQ, 128), BF16),
@@ -407,7 +412,7 @@
             pltpu.VMEM((8, REQ, 384), BF16),
             pltpu.VMEM((8, REQ, 256), BF16),
             pltpu.VMEM((8, REQ, 256), BF16),
-            dma((7,)),
+            dma((11,)),
             dma,
             dma((2, 4, 4)),
             dma,

time: 39.4 us -> 38.7 us (0.982)
  Pallas kernels: 37.5 us -> 36.8 us
    pallas_call x1, Pallas kernels: 37.5 us -> 36.8 us  [on_device(): pl.pallas_call(kernel, out_shape=(jax.ShapeDtypeStruct((REQ, 256), BF16),...]
where the time goes in v6:
time: 38.7 us; the launch traced here: 38.6 us
  Pallas kernels  36.8 us (95%)
  local copies, waits for them, and re-layouts  1.19 us (3%)
  between operations  0.64 us (2%)
    pallas_call x1, Pallas kernels, on_device(): pl.pallas_call(kernel, out_shape=(jax.ShapeDtypeStruct((REQ, 256), BF16),...  36.8 us
    unnamed x2, local copies, waits for them, and re-layouts  1.19 us

profile of v6, /device:TPU:1, one launch (start us, length us, event | category | flops | bytes accessed | tf_op | source)
XLA Modules:
  0.0 38.6 jit_solution(16425064255397697365)
XLA Ops:
  0.6 36.8 %shard_map.122 = (bf16[16,256]{1,0:T(8,128)(2,1)S(1)}, bf16[16,64]{1,0:T(8,128)(2,1)S(1)}) custom-call(bf16[16,2048]{1,0:T(8,128)(2,1)} %hid.1, bf16[2048]{0:T(1024)(128)(2,1)} %gain.1, bf16[2048,256]{1,0:T(8,128)(2,1)} %wq.1, bf16[64,2048]{1,0:T(8,128)(2,1)} %bitcast.1, bf16[256,2048]{1,0:T(8,128)(2,1)} %wo.1, bf16[2,64,512]{2,1,0:T(8,128)(2,1)} %prefix.1, ...), custom_call_target="tpu_custom_call" | custom-call | tf_op jit(solution)/shard_map/pallas_call | solution.py:388
  37.4 0.6 %copy.15 = bf16[16,256]{1,0:T(8,128)(2,1)} copy(bf16[16,256]{1,0:T(8,128)(2,1)S(1)} %get-tuple-element.4) | data formatting | bytes 16384
  38.0 0.6 %copy.16 = bf16[16,64]{1,0:T(8,128)(2,1)} copy(bf16[16,64]{1,0:T(8,128)(2,1)S(1)} %get-tuple-element.5) | data formatting | bytes 4096

commit v7 on v6

--- a/solution.py
+++ b/solution.py
@@ -86,7 +86,8 @@
          (prefix, chunk(x, y, c)), (parent_in, parent), (nlen_in, nlen), (reqnode_in, reqnode), (plen_in, plen))
     ):
         copy = pltpu.make_async_copy(src, dst, l_sem.at[k])
-        copy.start()
+        if k not in (4, 5, 6):
+            copy.start()
         locals_.append(copy)
 
     def send(src, dst, ssem, rsem, peer):
@@ -127,6 +128,8 @@
     hand_on(1, 0, 0, ("y", 2))
     hand_on(0, 0, 0, ("y", 1), ("y", -1), ("s", 0))
     hand_on(1, 0, 0, ("x", 1), ("x", -1), ("s", 0))
+    for k in (4, 5, 6):
+        locals_[k].start()
 
     for k in range(7, 11):
         locals_[k].wait()
@@ -362,14 +365,14 @@
             send(rs_send.at[to], rs_recv.at[t], z_send.at[2], z_recv.at[2], z_peer[d])
         else:
             rs_recv[t] = block
+    arrived(part_send.at[pl.ds(0, 7)], z_send.at[1])
+    arrived(rs_send.at[pl.ds(0, 7)], z_send.at[2])
     arrived(rs_recv.at[pl.ds(0, 7)], z_recv.at[2])
     result = v_hid[:, pl.ds(pl.multiple_of(t * 256, 256), 256)].astype(F32)
     for s in range(8):
         result = result + rs_recv[s].astype(F32)
     out_h[...] = result.astype(BF16)
 
-    arrived(part_send.at[pl.ds(0, 7)], z_send.at[1])
-    arrived(rs_send.at[pl.ds(0, 7)], z_send.at[2])
     for j in range(2):
         target = (t % KV_HEADS) * 2 + j
 

time: 38.7 us -> 38.7 us (level)
  no operation moved by 1% of the time
where the time goes in v7:
time: 38.7 us; the launch traced here: 38.6 us
  Pallas kernels  36.8 us (95%)
  local copies, waits for them, and re-layouts  1.19 us (3%)
  between operations  0.64 us (2%)
    pallas_call x1, Pallas kernels, on_device(): pl.pallas_call(kernel, out_shape=(jax.ShapeDtypeStruct((REQ, 256), BF16),...  36.8 us
    unnamed x2, local copies, waits for them, and re-layouts  1.19 us

profile of v7, /device:TPU:1, one launch (start us, length us, event | category | flops | bytes accessed | tf_op | source)
XLA Modules:
  0.0 38.6 jit_solution(9740262228556411336)
XLA Ops:
  0.6 36.8 %shard_map.122 = (bf16[16,256]{1,0:T(8,128)(2,1)S(1)}, bf16[16,64]{1,0:T(8,128)(2,1)S(1)}) custom-call(bf16[16,2048]{1,0:T(8,128)(2,1)} %hid.1, bf16[2048]{0:T(1024)(128)(2,1)} %gain.1, bf16[2048,256]{1,0:T(8,128)(2,1)} %wq.1, bf16[64,2048]{1,0:T(8,128)(2,1)} %bitcast.1, bf16[256,2048]{1,0:T(8,128)(2,1)} %wo.1, bf16[2,64,512]{2,1,0:T(8,128)(2,1)} %prefix.1, ...), custom_call_target="tpu_custom_call" | custom-call | tf_op jit(solution)/shard_map/pallas_call | solution.py:391
  37.4 0.6 %copy.15 = bf16[16,256]{1,0:T(8,128)(2,1)} copy(bf16[16,256]{1,0:T(8,128)(2,1)S(1)} %get-tuple-element.4) | data formatting | bytes 16384
  38.0 0.6 %copy.16 = bf16[16,64]{1,0:T(8,128)(2,1)} copy(bf16[16,64]{1,0:T(8,128)(2,1)S(1)} %get-tuple-element.5) | data formatting | bytes 4096
